TPU v7x, 256 devices: a whole 4x4x8 slice. The times are simulated.
256 devices in a mesh: dp: 16 (over y, z_hi), block: 16 (over z_lo, x, core).
Axes of the slice: x: 4, y: 4, z: 8 (z_hi: 4, z_lo: 2; z = z_hi * 2 + z_lo), core: 2. Of those that a mesh axis runs over, the one named last changes fastest.
Arguments:
- layer_input: bfloat16 [128, 128, 32768], P('block', None, 'dp'), may hold values from -6 to 6
- w_first: bfloat16 [128, 128, 128], P('block'), may hold values from -0.5 to 0.5
- w_second: bfloat16 [128, 128, 128], P('block'), may hold values from -0.5 to 0.5
- cotangent: bfloat16 [128, 128, 32768], P('block', None, 'dp'), may hold values from -6 to 6
Outputs:
- grad_input: bfloat16 [128, 128, 32768], P('block', None, 'dp')
- grad_first: float32 [128, 128, 128], P('block', 'dp')
- grad_second: float32 [128, 128, 128], P('block', 'dp')
- cov_in_first: float32 [128, 128, 128], P('block', 'dp')
- cov_out_first: float32 [128, 128, 128], P('block', 'dp')
- cov_in_second: float32 [128, 128, 128], P('block', 'dp')
- cov_out_second: float32 [128, 128, 128], P('block', 'dp')
All inputs are finite; a program needn't handle non-finite values.
Results may differ from a plain program's by a relative error of at most 0.0049.
Values may be sent and summed in bfloat16 or wider, within the bound.
No kernel may reach another device: no remote copies, remote signals or barrier semaphores. Data moves between devices by JAX's collectives and lax.ppermute only.
A program may use at most 128 MiB of HBM per device.

v0:
```python
import math

import jax
import jax.numpy as jnp
from jax import lax
from jax.sharding import PartitionSpec as P


def per_device(layer_input, w_first, w_second, cotangent):
    total = layer_input.shape[2] * lax.axis_size("dp")
    root = 1.0 / math.sqrt(total)
    scale = 1.0 / total
    hidden = jnp.einsum(
        "ikt,ikj->jit", layer_input, w_first, preferred_element_type=jnp.float32
    ).astype(jnp.bfloat16)
    mixed = lax.all_to_all(hidden, "block", split_axis=0, concat_axis=1, tiled=True)
    grad_second = (
        jnp.einsum("jit,jmt->jim", mixed, cotangent, preferred_element_type=jnp.float32) * root
    )
    cov_in_second = (
        jnp.einsum("jit,jlt->jil", mixed, mixed, preferred_element_type=jnp.float32) * scale
    )
    cov_out_second = (
        jnp.einsum("jmt,jnt->jmn", cotangent, cotangent, preferred_element_type=jnp.float32) * scale
    )
    grad_mixed = jnp.einsum(
        "jim,jmt->jit", w_second, cotangent, preferred_element_type=jnp.float32
    ).astype(jnp.bfloat16)
    grad_hidden = lax.all_to_all(grad_mixed, "block", split_axis=1, concat_axis=0, tiled=True)
    result = jnp.einsum(
        "ikj,jit->ikt", w_first, grad_hidden, preferred_element_type=jnp.float32
    ).astype(jnp.bfloat16)
    grad_hidden, grad_input = (grad_hidden, result)
    grad_first = (
        jnp.einsum("ikt,jit->ikj", layer_input, grad_hidden, preferred_element_type=jnp.float32)
        * root
    )
    cov_in_first = (
        jnp.einsum("ikt,ilt->ikl", layer_input, layer_input, preferred_element_type=jnp.float32)
        * scale
    )
    cov_out_first = (
        jnp.einsum("jit,lit->ijl", grad_hidden, grad_hidden, preferred_element_type=jnp.float32)
        * scale
    )
    summed = (
        lax.psum_scatter(grad_first, "dp", scatter_dimension=1, tiled=True),
        lax.psum_scatter(grad_second, "dp", scatter_dimension=1, tiled=True),
        lax.psum_scatter(cov_in_first, "dp", scatter_dimension=1, tiled=True),
        lax.psum_scatter(cov_out_first, "dp", scatter_dimension=1, tiled=True),
        lax.psum_scatter(cov_in_second, "dp", scatter_dimension=1, tiled=True),
        lax.psum_scatter(cov_out_second, "dp", scatter_dimension=1, tiled=True),
    )
    grad_first, grad_second, cov_in_first, cov_out_first, cov_in_second, cov_out_second = summed
    return (
        grad_input,
        grad_first,
        grad_second,
        cov_in_first,
        cov_out_first,
        cov_in_second,
        cov_out_second,
    )


def solution(mesh):
    in_specs = (
        P("block", None, "dp"),
        P("block", None, None),
        P("block", None, None),
        P("block", None, "dp"),
    )
    out_specs = (
        P("block", None, "dp"),
        P("block", "dp", None),
        P("block", "dp", None),
        P("block", "dp", None),
        P("block", "dp", None),
        P("block", "dp", None),
        P("block", "dp", None),
    )
    return jax.shard_map(
        per_device, mesh=mesh, in_specs=in_specs, out_specs=out_specs, check_vma=False
    )
```

profile of v0, /device:TPU:2, one launch (start us, length us, event | category | flops | bytes accessed | tf_op | source)
XLA Modules:
  0.0 638.4 jit_solution(12375189317160173727)
XLA Ops:
  7.2 3.6 convolution_convert_fusion
  10.7 4.3 copy.39
  15.0 6.5 %all-to-all-start = ((bf16[8,128,2048]{2,0,1:T(8,128)(2,1)}), bf16[8,128,2048]{2,0,1:T(8,128)(2,1)}, u32[]{:S(2)}, u32[]{:S(2)}) async-start(bf16[8,128,2048]{2,0,1:T(8,128)(2,1)} %copy.39), calls=%async_computation | async-start | bytes 8388608 | tf_op jit(solution)/shard_map/all_to_all | solution.py:29
  21.6 3.5 convert_bitcast_fusion
  25.1 4.3 copy.46
  29.4 52.0 %all-to-all-done = bf16[8,128,2048]{2,0,1:T(8,128)(2,1)} async-done(((bf16[8,128,2048]{2,0,1:T(8,128)(2,1)}), bf16[8,128,2048]{2,0,1:T(8,128)(2,1)}, u32[]{:S(2)}, u32[]{:S(2)}) %all-to-all-start) | async-done | bytes 4194336 | tf_op jit(solution)/shard_map/all_to_all | solution.py:29
  81.4 6.9 %all-to-all-start.1 = ((bf16[128,8,2048]{2,1,0:T(8,128)(2,1)}), bf16[128,8,2048]{2,1,0:T(8,128)(2,1)}, u32[]{:S(2)}, u32[]{:S(2)}) async-start(bf16[128,8,2048]{2,1,0:T(8,128)(2,1)} %copy.46), calls=%async_computation.2 | async-start | bytes 8388608 | tf_op jit(solution)/shard_map/all_to_all | solution.py:16
  88.2 0.2 reduce-scatter.7.cloned.1.call-start
  88.5 5.2 copy.41
  93.7 2.0 copy-done.2
  95.7 2.9 fusion.14
  98.5 1.0 copy.44
  99.6 0.0 reduce-scatter.11.cloned.1.call-start
  99.6 5.5 convolution_multiply_fusion.1
  105.2 0.0 reduce-scatter.17.cloned.1.call-start
  105.3 5.5 convolution_multiply_fusion
  110.8 0.3 reduce-scatter.13.cloned.1.call-start
  111.1 8.8 %fusion.17 = f32[8,128,128]{2,1,0:T(8,128)} fusion(bf16[128,8,2048]{2,1,0:T(8,128)(2,1)} %bitcast.34), kind=kOutput, calls=%fused_computation.18 | convolution fusion | flops 537001984 | bytes 4718592 | tf_op jit(solution)/shard_map/jit,lit->ijl/dot_general | solution.py:43
  119.8 0.0 reduce-scatter.15.cloned.1.call-start
  119.9 30.5 %all-to-all-done.1 = bf16[128,8,2048]{2,1,0:T(8,128)(2,1)} async-done(((bf16[128,8,2048]{2,1,0:T(8,128)(2,1)}), bf16[128,8,2048]{2,1,0:T(8,128)(2,1)}, u32[]{:S(2)}, u32[]{:S(2)}) %all-to-all-start.1) | async-done | bytes 4194336 | tf_op jit(solution)/shard_map/all_to_all | solution.py:16
  150.4 5.6 fusion.23
  156.0 0.3 reduce-scatter.9.cloned.1.call-start
  156.3 5.5 fusion.20
  161.8 8.9 %convert_bitcast_fusion.1 = bf16[8,128,2048]{1,2,0:T(8,128)(2,1)} fusion(bf16[8,128,128]{2,1,0:T(8,128)(2,1)S(1)} %copy-done, bf16[128,8,2048]{2,1,0:T(8,128)(2,1)} %bitcast.35), kind=kOutput, calls=%fused_computation.5 | convolution fusion | flops 538968064 | bytes 8650752 | tf_op jit(solution)/shard_map/ikj,jit->ikt/dot_general | solution.py:30
  170.7 6.4 %copy.50 = bf16[8,128,2048]{2,1,0:T(8,128)(2,1)} copy(bf16[8,128,2048]{1,2,0:T(8,128)(2,1)} %convert_bitcast_fusion.1) | data formatting | bytes 8388608
  177.2 12.1 %reduce-scatter.7.cloned.1.call-done = f32[8,8,128]{2,0,1:T(8,128)} async-done(((f32[8,128,128]{2,0,1:T(8,128)}), f32[8,8,128]{2,0,1:T(8,128)}) %reduce-scatter.7.cloned.1.call-update) | async-done | bytes 32784 | tf_op jit(solution)/shard_map/reduce_scatter | solution.py:47
  189.3 1.4 copy.51
  190.6 87.2 %reduce-scatter.11.cloned.1.call-done = f32[8,8,128]{2,1,0:T(8,128)} async-done(((f32[8,128,128]{2,1,0:T(8,128)}), f32[8,8,128]{2,1,0:T(8,128)}) %reduce-scatter.11.cloned.1.call-update) | async-done | bytes 32784 | tf_op jit(solution)/shard_map/reduce_scatter | solution.py:49
  277.8 88.5 %reduce-scatter.17.cloned.1.call-done = f32[8,8,128]{2,1,0:T(8,128)} async-done(((f32[8,128,128]{2,1,0:T(8,128)}), f32[8,8,128]{2,1,0:T(8,128)}) %reduce-scatter.17.cloned.1.call-update) | async-done | bytes 32784 | tf_op jit(solution)/shard_map/reduce_scatter | solution.py:52
  366.4 88.4 %reduce-scatter.13.cloned.1.call-done = f32[8,8,128]{2,1,0:T(8,128)} async-done(((f32[8,128,128]{2,1,0:T(8,128)}), f32[8,8,128]{2,1,0:T(8,128)}) %reduce-scatter.13.cloned.1.call-update) | async-done | bytes 32784 | tf_op jit(solution)/shard_map/reduce_scatter | solution.py:50
  454.8 88.4 %reduce-scatter.15.cloned.1.call-done = f32[8,8,128]{2,1,0:T(8,128)} async-done(((f32[8,128,128]{2,1,0:T(8,128)}), f32[8,8,128]{2,1,0:T(8,128)}) %reduce-scatter.15.cloned.1.call-update) | async-done | bytes 32784 | tf_op jit(solution)/shard_map/reduce_scatter | solution.py:51
  543.2 88.4 %reduce-scatter.9.cloned.1.call-done = f32[8,8,128]{2,1,0:T(8,128)} async-done(((f32[8,128,128]{2,1,0:T(8,128)}), f32[8,8,128]{2,1,0:T(8,128)}) %reduce-scatter.9.cloned.1.call-update) | async-done | bytes 32784 | tf_op jit(solution)/shard_map/reduce_scatter | solution.py:48
  (11 shorter events, 0.1 us)
Async XLA Ops:
  7.2 14.4 %copy-start = (bf16[8,128,128]{2,1,0:T(8,128)(2,1)S(1)}, bf16[8,128,128]{2,1,0:T(8,128)(2,1)}, u32[]{:S(2)}) copy-start(bf16[8,128,128]{2,1,0:T(8,128)(2,1)} %param.5) | copy-start | bytes 786436
  15.0 66.3 %all-to-all-start = ((bf16[8,128,2048]{2,0,1:T(8,128)(2,1)}), bf16[8,128,2048]{2,0,1:T(8,128)(2,1)}, u32[]{:S(2)}, u32[]{:S(2)}) async-start(bf16[8,128,2048]{2,0,1:T(8,128)(2,1)} %copy.39), calls=%async_computation | async-start | bytes 8388608 | tf_op jit(solution)/shard_map/all_to_all | solution.py:29
  81.4 69.0 %all-to-all-start.1 = ((bf16[128,8,2048]{2,1,0:T(8,128)(2,1)}), bf16[128,8,2048]{2,1,0:T(8,128)(2,1)}, u32[]{:S(2)}, u32[]{:S(2)}) async-start(bf16[128,8,2048]{2,1,0:T(8,128)(2,1)} %copy.46), calls=%async_computation.2 | async-start | bytes 8388608 | tf_op jit(solution)/shard_map/all_to_all | solution.py:16
  88.2 101.0 %reduce-scatter.7.cloned.1.call-start = ((), (), s32[]{:S(2)}) async-start(), calls=%async_computation.8 | async-start | bytes 557056 | tf_op jit(solution)/shard_map/reduce_scatter | solution.py:47
  88.5 7.2 %copy-start.1 = (bf16[8,128,2048]{2,1,0:T(8,128)(2,1)S(1)}, bf16[8,128,2048]{2,1,0:T(8,128)(2,1)}, u32[]{:S(2)}) copy-start(bf16[8,128,2048]{2,1,0:T(8,128)(2,1)} %param.4) | copy-start | bytes 12582916
  93.6 2.0 copy-start.2
  99.6 178.2 %reduce-scatter.11.cloned.1.call-start = ((), (), s32[]{:S(2)}) async-start(), calls=%async_computation.10 | async-start | bytes 557056 | tf_op jit(solution)/shard_map/reduce_scatter | solution.py:49
  105.2 261.1 %reduce-scatter.17.cloned.1.call-start = ((), (), s32[]{:S(2)}) async-start(), calls=%async_computation.13 | async-start | bytes 557056 | tf_op jit(solution)/shard_map/reduce_scatter | solution.py:52
  110.8 344.0 %reduce-scatter.13.cloned.1.call-start = ((), (), s32[]{:S(2)}) async-start(), calls=%async_computation.11 | async-start | bytes 557056 | tf_op jit(solution)/shard_map/reduce_scatter | solution.py:50
  119.8 423.3 %reduce-scatter.15.cloned.1.call-start = ((), (), s32[]{:S(2)}) async-start(), calls=%async_computation.12 | async-start | bytes 557056 | tf_op jit(solution)/shard_map/reduce_scatter | solution.py:51
  156.0 475.6 %reduce-scatter.9.cloned.1.call-start = ((), (), s32[]{:S(2)}) async-start(), calls=%async_computation.9 | async-start | bytes 557056 | tf_op jit(solution)/shard_map/reduce_scatter | solution.py:48
Sparse Core Ops, SparseCore 0:
  99.7 89.5 reduce-scatter.6
  193.3 84.4 reduce-scatter.10
  281.9 84.4 reduce-scatter.16
  370.3 84.4 reduce-scatter.12
  458.7 84.4 reduce-scatter.14
  547.1 84.4 reduce-scatter.8
where the time goes:
time: 639 us; the launch traced here: 638 us
  waiting for transfers between devices  536 us (84%)
  matrix products  49.6 us (8%)
  local copies, waits for them, and re-layouts  24.6 us (4%)
  starting transfers between devices  14.3 us (2%)
  between operations  14.2 us (2%)
    reduce_scatter x1, waiting for transfers between devices, per_device(): lax.psum_scatter(cov_out_second, 'dp', scatter_dimension=1, tiled=True)  88.5 us
    reduce_scatter x1, waiting for transfers between devices, per_device(): lax.psum_scatter(cov_out_first, 'dp', scatter_dimension=1, tiled=True)  88.4 us
    reduce_scatter x1, waiting for transfers between devices, per_device(): lax.psum_scatter(grad_second, 'dp', scatter_dimension=1, tiled=True)  88.4 us
    reduce_scatter x1, waiting for transfers between devices, per_device(): lax.psum_scatter(cov_in_second, 'dp', scatter_dimension=1, tiled=True)  88.4 us
    reduce_scatter x1, waiting for transfers between devices, per_device(): lax.psum_scatter(cov_in_first, 'dp', scatter_dimension=1, tiled=True)  87.2 us
    all_to_all x1, waiting for transfers between devices, per_device(): lax.all_to_all(grad_mixed, 'block', split_axis=1, concat_axis=0, tiled=True)  52 us
    all_to_all x1, waiting for transfers between devices, per_device(): lax.all_to_all(hidden, 'block', split_axis=0, concat_axis=1, tiled=True)  30.5 us
  transfers between devices with their start and end apart: 8, of which 8 were waited for; matrix products, arithmetic and copies ran while one was open for 10% of the time, Pallas kernels for 0%

commit v1 on v0

v1 whole, which is shorter than its diff:
```python
import functools
import math

import jax
import jax.numpy as jnp
from jax import lax
from jax.experimental import pallas as pl
from jax.experimental.pallas import tpu as pltpu
from jax.sharding import PartitionSpec as P


BF = jnp.bfloat16
F32 = jnp.float32
VMEM = pltpu.MemorySpace.VMEM
SMEM = pltpu.MemorySpace.SMEM
NT = (((1,), (1,)), ((), ()))


def params(mib):
    return pltpu.CompilerParams(vmem_limit_bytes=mib << 20)


def cost(flops, moved):
    return pl.CostEstimate(flops=flops, bytes_accessed=moved, transcendentals=0)


def in_hbm(v):
    return pltpu.with_memory_space_constraint(v, pltpu.HBM)


def fetch(src, dst, sems, b):
    return pltpu.make_async_copy(src.at[b], dst.at[b], sems.at[b])


def mix(weights_at, n, me, wbuf):
    for k in range(n):
        wbuf[k] = weights_at(me ^ k)
    a, b, c = wbuf.shape
    return wbuf[...].reshape(a * b, c)


def send_g_kernel(me_ref, w_ref, c_hbm, *refs):
    n = w_ref.shape[1]
    outs, (cbuf, wall, wbuf, sems, wsem) = refs[:n], refs[n:]
    nb, _, rows, _ = w_ref.shape
    me = me_ref[0]
    weights = pltpu.make_async_copy(w_ref, wall, wsem)
    weights.start()
    for j in range(nb):
        fetch(c_hbm, cbuf, sems, j).start()
    weights.wait()

    def step(j, carry):
        w = mix(lambda d: wall[j, d], n, me, wbuf)
        fetch(c_hbm, cbuf, sems, j).wait()
        r = jnp.dot(w, cbuf[j], preferred_element_type=F32)
        for k in range(n):
            outs[k][j] = r[k * rows : (k + 1) * rows].astype(BF)
        return carry

    lax.fori_loop(0, nb, step, 0)


def send_g(me, w_second, cotangent, n):
    nb, bs, t = cotangent.shape
    rows = bs // n
    return pl.pallas_call(
        send_g_kernel,
        in_specs=[
            pl.BlockSpec(memory_space=SMEM),
            pl.BlockSpec(memory_space=pltpu.HBM),
            pl.BlockSpec(memory_space=pltpu.HBM),
        ],
        out_specs=[pl.BlockSpec(memory_space=VMEM)] * n,
        out_shape=[pltpu.VMEM((nb, rows, t), BF)] * n,
        scratch_shapes=[
            pltpu.VMEM((nb, bs, t), BF),
            pltpu.VMEM((nb, n, rows, bs), BF),
            pltpu.VMEM((n, rows, bs), BF),
            pltpu.SemaphoreType.DMA((nb,)),
            pltpu.SemaphoreType.DMA,
        ],
        compiler_params=params(12),
        cost_estimate=cost(2 * nb * bs * bs * t, 4 * nb * bs * t),
    )(me, in_hbm(w_second.reshape(nb, n, rows, bs)), in_hbm(cotangent))


def swap_matrix(rows):
    r = lax.broadcasted_iota(jnp.int32, (rows * rows, rows * rows), 0)
    c = lax.broadcasted_iota(jnp.int32, (rows * rows, rows * rows), 1)
    return jnp.where((r % rows) * rows + r // rows == c, 1.0, 0.0).astype(BF)


def swap(p, v):
    a, b, t = v.shape
    return jnp.dot(p, v.reshape(a * b, t), preferred_element_type=F32)


def send_h_kernel(n, me_ref, w_ref, x_hbm, *refs):
    outs, (xbuf, wbuf, wt, hid, sems) = refs[:n], refs[n:]
    nb, bs, _ = w_ref.shape
    rows = bs // n
    me = me_ref[0]
    for i in range(nb):
        fetch(x_hbm, xbuf, sems, i).start()

    def step(i, carry):
        wt[...] = w_ref[i].astype(F32).T.reshape(n, rows, bs).astype(BF)
        w = mix(lambda d: wt[d], n, me, wbuf)
        fetch(x_hbm, xbuf, sems, i).wait()
        r = jnp.dot(w, xbuf[i], preferred_element_type=F32)
        for k in range(n):
            hid[k, i] = r[k * rows : (k + 1) * rows].astype(BF)
        return carry

    lax.fori_loop(0, nb, step, 0)
    p = swap_matrix(rows)
    for k in range(n):
        s = swap(p, hid[k])
        for j in range(rows):
            outs[k][j] = s[j * nb : (j + 1) * nb].astype(BF)


def send_h(me, w_first, layer_input, n):
    nb, bs, t = layer_input.shape
    rows = bs // n
    return pl.pallas_call(
        functools.partial(send_h_kernel, n),
        in_specs=[
            pl.BlockSpec(memory_space=SMEM),
            pl.BlockSpec(memory_space=VMEM),
            pl.BlockSpec(memory_space=pltpu.HBM),
        ],
        out_specs=[pl.BlockSpec(memory_space=VMEM)] * n,
        out_shape=[pltpu.VMEM((rows, nb, t), BF)] * n,
        scratch_shapes=[
            pltpu.VMEM((nb, bs, t), BF),
            pltpu.VMEM((n, rows, bs), BF),
            pltpu.VMEM((n, rows, bs), BF),
            pltpu.VMEM((n, nb, rows, t), BF),
            pltpu.SemaphoreType.DMA((nb,)),
        ],
        compiler_params=params(16),
        cost_estimate=cost(4 * nb * bs * bs * t, 4 * nb * bs * t),
    )(me, w_first, in_hbm(layer_input))


NY = 4
ORDER = (10, 6, 14, 2, 8, 4, 12, 11, 7, 15, 3, 9, 5, 13, 1)
ISSUE = (0,) + ORDER


def put(o_refs, buf, me_ref, which, b, value):
    keep, send = o_refs
    half, nh, _, _, rows, bs = keep.shape
    buf[...] = value.reshape(2, half, nh, rows, bs)
    high = lax.div(me_ref[1], half * nh)
    keep[:, :, which, b] = buf[high]
    send[:, :, which, b] = buf[1 - high].astype(BF)


def local_stats_kernel(scale, me_ref, x_ref, c_ref, *refs):
    o_refs, buf = refs[:2], refs[2]
    b = pl.program_id(0)
    x = x_ref[0]
    c = c_ref[0]
    put(o_refs, buf, me_ref, 0, b, lax.dot_general(x, x, NT, preferred_element_type=F32) * scale)
    put(o_refs, buf, me_ref, 1, b, lax.dot_general(c, c, NT, preferred_element_type=F32) * scale)


def pieces_of(nb, bs, d):
    nh = d // NY
    shape = (NY // 2, nh, 2, nb, bs // d, bs)
    spec = pl.BlockSpec(shape, lambda b: (0, 0, 0, 0, 0, 0))
    buf = pltpu.VMEM((2, NY // 2, nh, bs // d, bs), F32)
    return [spec] * 2, [jax.ShapeDtypeStruct(shape, F32), jax.ShapeDtypeStruct(shape, BF)], buf


def local_stats(me, layer_input, cotangent, scale, d):
    nb, bs, t = layer_input.shape
    out_specs, out_shape, buf = pieces_of(nb, bs, d)
    spec = pl.BlockSpec((1, bs, t), lambda b: (b, 0, 0))
    return pl.pallas_call(
        functools.partial(local_stats_kernel, scale),
        grid=(nb,),
        in_specs=[pl.BlockSpec(memory_space=SMEM), spec, spec],
        out_specs=out_specs,
        out_shape=out_shape,
        scratch_shapes=[buf],
        compiler_params=params(8),
        cost_estimate=cost(4 * nb * bs * bs * t, 4 * nb * bs * t),
    )(me, layer_input, cotangent)


def first_kernel(scale, root, n, me_ref, w_ref, x_ref, *refs):
    got = [refs[ISSUE.index(k)] for k in range(n)]
    gi_ref, o_refs, (grad, buf) = refs[n], refs[n + 1 : n + 3], refs[n + 3 :]
    nb = got[0].shape[1]
    rows = got[0].shape[0]
    me = me_ref[0]
    i = pl.program_id(0)

    @pl.when(i == 0)
    def _():
        p = swap_matrix(rows)
        for k in range(n):
            s = swap(p, got[k][...])
            for b in range(nb):
                grad[b, me ^ k] = s[b * rows : (b + 1) * rows].astype(BF)

    g = grad[i]
    g = g.reshape(g.shape[0] * g.shape[1], g.shape[2])
    x = x_ref[0]
    gi_ref[0] = jnp.dot(w_ref[0], g, preferred_element_type=F32).astype(BF)
    put(o_refs, buf, me_ref, 0, i, lax.dot_general(x, g, NT, preferred_element_type=F32) * root)
    put(o_refs, buf, me_ref, 1, i, lax.dot_general(g, g, NT, preferred_element_type=F32) * scale)


def first_block(me, w_first, layer_input, got, scale, root, d):
    n = len(got)
    nb, bs, t = layer_input.shape
    out_specs, out_shape, buf = pieces_of(nb, bs, d)
    return pl.pallas_call(
        functools.partial(first_kernel, scale, root, n),
        grid=(nb,),
        in_specs=[
            pl.BlockSpec(memory_space=SMEM),
            pl.BlockSpec((1, bs, bs), lambda i: (i, 0, 0)),
            pl.BlockSpec((1, bs, t), lambda i: (i, 0, 0)),
        ]
        + [pl.BlockSpec(memory_space=VMEM)] * n,
        out_specs=[pl.BlockSpec((1, bs, t), lambda i: (i, 0, 0))] + out_specs,
        out_shape=[jax.ShapeDtypeStruct((nb, bs, t), BF)] + out_shape,
        scratch_shapes=[pltpu.VMEM((nb, n, bs // n, t), BF), buf],
        compiler_params=params(16),
        cost_estimate=cost(8 * nb * bs * bs * t, 6 * nb * bs * t),
    )(me, w_first, layer_input, *[got[k] for k in ISSUE])


def second_kernel(scale, root, n, me_ref, c_ref, *refs):
    got = [refs[ISSUE.index(k)] for k in range(n)]
    o_ref, mixed = refs[n:]
    me = me_ref[0]
    j = pl.program_id(0)
    for k in range(n):
        mixed[me ^ k] = got[k][j]
    m = mixed[...]
    m = m.reshape(m.shape[0] * m.shape[1], m.shape[2])
    d, _, _, rows, bs = o_ref.shape
    cov = lax.dot_general(m, m, NT, preferred_element_type=F32) * scale
    grad = lax.dot_general(m, c_ref[0], NT, preferred_element_type=F32) * root
    o_ref[:, 0, j] = cov.reshape(d, rows, bs).astype(BF)
    o_ref[:, 1, j] = grad.reshape(d, rows, bs).astype(BF)


def second_block(me, cotangent, got, scale, root, d):
    n = len(got)
    nb, bs, t = cotangent.shape
    shape = (d, 2, nb, bs // d, bs)
    return pl.pallas_call(
        functools.partial(second_kernel, scale, root, n),
        grid=(nb,),
        in_specs=[
            pl.BlockSpec(memory_space=SMEM),
            pl.BlockSpec((1, bs, t), lambda j: (j, 0, 0)),
        ]
        + [pl.BlockSpec(memory_space=VMEM)] * n,
        out_specs=pl.BlockSpec(shape, lambda j: (0, 0, 0, 0, 0)),
        out_shape=jax.ShapeDtypeStruct(shape, BF),
        scratch_shapes=[pltpu.VMEM((n, bs // n, t), BF)],
        compiler_params=params(8),
        cost_estimate=cost(4 * nb * bs * bs * t, 4 * nb * bs * t),
    )(me, cotangent, *[got[k] for k in ISSUE])


def exchange(pieces):
    n = len(pieces)
    got = list(pieces)
    for k in ORDER:
        got[k] = lax.ppermute(pieces[k], "block", [(p, p ^ k) for p in range(n)])
    return [pltpu.with_memory_space_constraint(v, pltpu.VMEM) for v in got]


def halve_kernel(bit, sets, me_ref, *refs):
    keep, send, buf = refs[2 * sets :]
    width = buf.shape[-4] // sets
    for s in range(sets):
        total = refs[2 * s][...] + refs[2 * s + 1][...].astype(F32)
        if sets == 1:
            buf[...] = total.reshape(buf.shape)
        else:
            buf[:, :, s * width : (s + 1) * width] = total
    mine = lax.rem(lax.div(me_ref[1], bit), 2)
    keep[...] = buf[mine]
    send[...] = buf[1 - mine].astype(BF)


def halve(me, bit, *sets):
    shape = list(sets[0][0].shape)
    shape[-4] *= len(sets)
    if shape[0] != 2:
        shape = [2, shape[0] // 2] + shape[1:]
    elif len(shape) == 5:
        shape = [2] + shape[1:]
    out = tuple(shape[1:])
    flat = [v for pair in sets for v in pair]
    return pl.pallas_call(
        functools.partial(halve_kernel, bit, len(sets)),
        in_specs=[pl.BlockSpec(memory_space=SMEM)] + [pl.BlockSpec(memory_space=VMEM)] * len(flat),
        out_specs=[pl.BlockSpec(memory_space=VMEM)] * 2,
        out_shape=[jax.ShapeDtypeStruct(out, F32), jax.ShapeDtypeStruct(out, BF)],
        scratch_shapes=[pltpu.VMEM(tuple(shape), F32)],
        compiler_params=params(12),
        cost_estimate=cost(2 * flat[0].size, 12 * flat[0].size),
    )(me, *flat)


def swap_dp(v, bit):
    d = lax.axis_size("dp")
    return lax.ppermute(v, "dp", [(p, p ^ bit) for p in range(d)])


def finish_kernel(v_ref, keep_ref, got_ref, *o_refs):
    total = v_ref[0].astype(F32)
    for k in range(1, v_ref.shape[0]):
        total = total + v_ref[k].astype(F32)
    for s in range(total.shape[0]):
        o_refs[s][...] = total[s]
    rest = keep_ref[...] + got_ref[...].astype(F32)
    for s in range(rest.shape[0]):
        o_refs[total.shape[0] + s][...] = rest[s]


def finish(v, keep, got):
    shape = v.shape[2:]
    outs = v.shape[1] + keep.shape[0]
    return pl.pallas_call(
        finish_kernel,
        in_specs=[pl.BlockSpec(memory_space=VMEM)] * 3,
        out_specs=[pl.BlockSpec(memory_space=VMEM)] * outs,
        out_shape=[jax.ShapeDtypeStruct(shape, F32)] * outs,
        compiler_params=params(6),
        cost_estimate=cost(2 * v.size, 6 * v.size),
    )(v, keep, got)


def per_device(layer_input, w_first, w_second, cotangent):
    _, _, t = layer_input.shape
    n = lax.axis_size("block")
    d = lax.axis_size("dp")
    total = t * d
    root = 1.0 / math.sqrt(total)
    scale = 1.0 / total
    me = jnp.stack([lax.axis_index("block"), lax.axis_index("dp")]).astype(jnp.int32)

    def after(v, *done):
        return lax.optimization_barrier((v,) + done)[0]

    def after(v, *done):
        return lax.optimization_barrier((v,) + done)[0]

    out_g = send_g(me, w_second, cotangent, n)
    got_g = exchange(out_g)
    out_h = send_h(me, w_first, after(layer_input, out_g[0]), n)
    got_h = exchange(out_h)
    local = local_stats(me, after(layer_input, out_h[0]), cotangent, scale, d)
    local_got = swap_dp(local[1], d // 2)
    x3 = after(layer_input, local[0])
    grad_input, *first = first_block(me, w_first, x3, got_g, scale, root, d)
    first_got = swap_dp(first[1], d // 2)
    keep, send = halve(me, d // 4, (local[0], local_got), (first[0], first_got))
    got = swap_dp(send, d // 4)
    keep, send = halve(me, d // 8, (keep, got))
    got = swap_dp(send, d // 8)
    second = second_block(me, cotangent, got_h, scale, root, d)
    keep, send = halve(me, d // 16, (keep, got))
    got = swap_dp(send, d // 16)
    second = lax.all_to_all(second, "dp", 0, 0, tiled=True)
    cov2, grad2, cov_in1, cov_out2, grad1, cov_out1 = finish(second, keep, got)
    return (grad_input, grad1, grad2, cov_in1, cov_out1, cov2, cov_out2)


def solution(mesh):
    in_specs = (
        P("block", None, "dp"),
        P("block", None, None),
        P("block", None, None),
        P("block", None, "dp"),
    )
    out_specs = (
        P("block", None, "dp"),
        P("block", "dp", None),
        P("block", "dp", None),
        P("block", "dp", None),
        P("block", "dp", None),
        P("block", "dp", None),
        P("block", "dp", None),
    )
    return jax.shard_map(
        per_device, mesh=mesh, in_specs=in_specs, out_specs=out_specs, check_vma=False
    )
```

time: 639 us -> 176 us (0.28)
  waiting for transfers between devices: 536 us -> 66.9 us
  starting transfers between devices: 14.3 us -> 70 us
  matrix products: 49.6 us -> 0 us
  Pallas kernels: 0 us -> 33 us
  local copies, waits for them, and re-layouts: 24.6 us -> 5.08 us
  between operations: 14.2 us -> 0.82 us
    reduce_scatter x6 -> x0, waiting for transfers between devices: 453 us -> none  [the longest x1 88.5 us: per_device(): lax.psum_scatter(cov_out_second, 'dp', scatter_dimension=1, tiled=True)]
    all_to_all x2 -> x1, waiting for transfers between devices: 82.5 us -> 0.01 us  [per_device(): second = lax.all_to_all(second, 'dp', 0, 0, tiled=True)]
    ppermute x0 -> x35, waiting for transfers between devices: none -> 66.9 us  [the longest x30 43.6 us: exchange(): got[k] = lax.ppermute(pieces[k], 'block', [(p, p ^ k) for p in range(n)])]
    ppermute x0 -> x35, starting transfers between devices: none -> 63 us  [the longest x30 50.6 us: exchange(): got[k] = lax.ppermute(pieces[k], 'block', [(p, p ^ k) for p in range(n)])]
    dot_general x9 -> x0, matrix products: 49.6 us -> none  [the longest x1 8.88 us: per_device(): jnp.einsum('ikj,jit->ikt', w_first, grad_hidden, preferred_element_type=j...]
    pallas_call x0 -> x9, Pallas kernels: none -> 33 us  [the longest x1 8.15 us: first_block(): pl.pallas_call(functools.partial(first_kernel, scale, root, n), grid=(nb,...]
    convert_element_type x2 -> x0, local copies, waits for them, and re-layouts: 8.59 us -> none  [the longest x1 4.31 us: per_device(): grad_mixed = jnp.einsum('jim,jmt->jit', w_second, cotangent, preferred_el...]
    all_to_all x2 -> x1, starting transfers between devices: 13.4 us -> 6.97 us  [per_device(): second = lax.all_to_all(second, 'dp', 0, 0, tiled=True)]
  transfers between devices with their start and end apart: 8 -> 36, of which waited for: 8 -> 12; matrix products, arithmetic and copies ran while one was open for 10% -> 0% of each run, Pallas kernels for 0% -> 15%
where the time goes in v1:
time: 176 us
  starting transfers between devices  70 us (40%)
  waiting for transfers between devices  66.9 us (38%)
  Pallas kernels  33 us (19%)
  local copies, waits for them, and re-layouts  5.08 us (3%)
    ppermute x30, starting transfers between devices, exchange(): got[k] = lax.ppermute(pieces[k], 'block', [(p, p ^ k) for p in range(n)])  50.6 us
    ppermute x30, waiting for transfers between devices, exchange(): got[k] = lax.ppermute(pieces[k], 'block', [(p, p ^ k) for p in range(n)])  43.6 us
    ppermute x5, waiting for transfers between devices, swap_dp(): return lax.ppermute(v, 'dp', [(p, p ^ bit) for p in range(d)])  23.3 us
    ppermute x5, starting transfers between devices, swap_dp(): return lax.ppermute(v, 'dp', [(p, p ^ bit) for p in range(d)])  12.4 us
    pallas_call x1, Pallas kernels, first_block(): pl.pallas_call(functools.partial(first_kernel, scale, root, n), grid=(nb,...  8.15 us
    all_to_all x1, starting transfers between devices, per_device(): second = lax.all_to_all(second, 'dp', 0, 0, tiled=True)  6.97 us
    pallas_call x1, Pallas kernels, send_g(): pl.pallas_call(send_g_kernel, in_specs=[pl.BlockSpec(memory_space=SMEM),...  6.64 us
    pallas_call x1, Pallas kernels, send_h(): pl.pallas_call(functools.partial(send_h_kernel, n), in_specs=[pl.BlockSpe...  6.01 us
  transfers between devices with their start and end apart: 36, of which 12 were waited for; matrix products, arithmetic and copies ran while one was open for 0% of the time, Pallas kernels for 15%

profile of v1, /device:TPU:2, one launch (start us, length us, event | category | flops | bytes accessed | tf_op | source)
XLA Modules:
  0.0 175.9 jit_solution(13630129392175890703)
XLA Ops:
  0.7 6.6 %shard_map.99 = (bf16[8,8,2048]{2,1,0:T(8,128)(2,1)S(1)}, bf16[8,8,2048]{2,1,0:T(8,128)(2,1)}, bf16[8,8,2048]{2,1,0:T(8,128)(2,1)S(1)}, bf16[8,8,2048]{2,1,0:T(8...) custom-call(s32[2]{0:T(128)S(1)} %pad_add_fusion.me_ref, ...), custom_call_target="tpu_custom_call" | custom-call | flops 536870912 | bytes 8388608 | tf_op jit(solution)/shard_map/pallas_call | solution.py:67
  9.3 2.2 %collective-permute-start.1 = (bf16[8,8,2048]{2,1,0:T(8,128)(2,1)S(1)}, bf16[8,8,2048]{2,1,0:T(8,128)(2,1)S(1)}, u32[]{:S(2)}, u32[]{:S(2)}) collective-permute-start(bf16[8,8,2048]{2,1,0:T(8,128)(2,1)S(1)} %get-tuple-element.66), channel_id=1, source_target_pairs={{0,6},{1,7},{2,4},{3,5},{4,2},{5,3},{6,0},{7,1},{8,14},{9,15},{10,... | collective-permute-start | bytes 786440 | tf_op jit(solution)/shard_map/ppermute | solution.py:280
  15.5 2.0 %collective-permute-done.refs_1_ = bf16[8,8,2048]{2,1,0:T(8,128)(2,1)S(1)} collective-permute-done((bf16[8,8,2048]{2,1,0:T(8,128)(2,1)S(1)}, bf16[8,8,2048]{2,1,0:T(8,128)(2,1)S(1)}, u32[]{:S(2)}, u32[]{:S(2)}) %collective-permute-start) | collective-permute-done | bytes 262176 | tf_op jit(solution)/shard_map/ppermute | solution.py:280
  17.6 2.1 %collective-permute-start.5 = (bf16[8,8,2048]{2,1,0:T(8,128)(2,1)S(1)}, bf16[8,8,2048]{2,1,0:T(8,128)(2,1)S(1)}, u32[]{:S(2)}, u32[]{:S(2)}) collective-permute-start(bf16[8,8,2048]{2,1,0:T(8,128)(2,1)S(1)} %get-tuple-element.70), channel_id=1, source_target_pairs={{0,4},{1,5},{2,6},{3,7},{4,0},{5,1},{6,2},{7,3},{8,12},{9,13},{10,... | collective-permute-start | bytes 786440 | tf_op jit(solution)/shard_map/ppermute | solution.py:280
  19.7 11.2 %collective-permute-done.1.refs_2_ = bf16[8,8,2048]{2,1,0:T(8,128)(2,1)S(1)} collective-permute-done((bf16[8,8,2048]{2,1,0:T(8,128)(2,1)S(1)}, bf16[8,8,2048]{2,1,0:T(8,128)(2,1)S(1)}, u32[]{:S(2)}, u32[]{:S(2)}) %collective-permute-start.1) | collective-permute-done | bytes 262176 | tf_op jit(solution)/shard_map/ppermute | solution.py:280
  30.9 3.5 %collective-permute-start.6 = (bf16[8,8,2048]{2,1,0:T(8,128)(2,1)S(1)}, bf16[8,8,2048]{2,1,0:T(8,128)(2,1)S(1)}, u32[]{:S(2)}, u32[]{:S(2)}) collective-permute-start(bf16[8,8,2048]{2,1,0:T(8,128)(2,1)S(1)} %get-tuple-element.71), channel_id=1, source_target_pairs={{0,12},{1,13},{2,14},{3,15},{4,8},{5,9},{6,10},{7,11},{8,4},{9,5},... | collective-permute-start | bytes 786440 | tf_op jit(solution)/shard_map/ppermute | solution.py:280
  35.6 6.0 %shard_map.100 = (bf16[8,8,2048]{2,1,0:T(8,128)(2,1)S(1)}, bf16[8,8,2048]{2,1,0:T(8,128)(2,1)S(1)}, bf16[8,8,2048]{2,1,0:T(8,128)(2,1)S(1)}, bf16[8,8,2048]{2,1,...) custom-call(s32[2]{0:T(128)S(1)} %pad_add_fusion.me_ref, ...), custom_call_target="tpu_custom_call" | custom-call | flops 1073741824 | bytes 8388608 | tf_op jit(solution)/shard_map/pallas_call | solution.py:127
  41.6 4.1 %collective-permute-start.15 = (bf16[8,8,2048]{2,1,0:T(8,128)(2,1)S(1)}, bf16[8,8,2048]{2,1,0:T(8,128)(2,1)S(1)}, u32[]{:S(2)}, u32[]{:S(2)}) collective-permute-start(bf16[8,8,2048]{2,1,0:T(8,128)(2,1)S(1)} %get-tuple-element.81), channel_id=1, source_target_pairs={{0,10},{1,11},{2,8},{3,9},{4,14},{5,15},{6,12},{7,13},{8,2},{9,3},... | collective-permute-start | bytes 786440 | tf_op jit(solution)/shard_map/ppermute | solution.py:280
  45.9 2.6 %collective-permute-start.17 = (bf16[8,8,2048]{2,1,0:T(8,128)(2,1)S(1)}, bf16[8,8,2048]{2,1,0:T(8,128)(2,1)S(1)}, u32[]{:S(2)}, u32[]{:S(2)}) collective-permute-start(bf16[8,8,2048]{2,1,0:T(8,128)(2,1)S(1)} %get-tuple-element.83), channel_id=1, source_target_pairs={{0,14},{1,15},{2,12},{3,13},{4,10},{5,11},{6,8},{7,9},{8,6},{9,7},... | collective-permute-start | bytes 786440 | tf_op jit(solution)/shard_map/ppermute | solution.py:280
  48.5 2.1 %collective-permute-done.8.refs_9_ = bf16[8,8,2048]{2,1,0:T(8,128)(2,1)S(1)} collective-permute-done((bf16[8,8,2048]{2,1,0:T(8,128)(2,1)S(1)}, bf16[8,8,2048]{2,1,0:T(8,128)(2,1)S(1)}, u32[]{:S(2)}, u32[]{:S(2)}) %collective-permute-start.8) | collective-permute-done | bytes 262176 | tf_op jit(solution)/shard_map/ppermute | solution.py:280
  50.5 3.3 %collective-permute-start.18 = (bf16[8,8,2048]{2,1,0:T(8,128)(2,1)S(1)}, bf16[8,8,2048]{2,1,0:T(8,128)(2,1)S(1)}, u32[]{:S(2)}, u32[]{:S(2)}) collective-permute-start(bf16[8,8,2048]{2,1,0:T(8,128)(2,1)S(1)} %get-tuple-element.84), channel_id=1, source_target_pairs={{0,2},{1,3},{2,0},{3,1},{4,6},{5,7},{6,4},{7,5},{8,10},{9,11},{10,... | collective-permute-start | bytes 786440 | tf_op jit(solution)/shard_map/ppermute | solution.py:280
  54.6 5.3 %collective-permute-done.15.refs_1_ = bf16[8,8,2048]{2,1,0:T(8,128)(2,1)S(1)} collective-permute-done((bf16[8,8,2048]{2,1,0:T(8,128)(2,1)S(1)}, bf16[8,8,2048]{2,1,0:T(8,128)(2,1)S(1)}, u32[]{:S(2)}, u32[]{:S(2)}) %collective-permute-start.15) | collective-permute-done | bytes 262176 | tf_op jit(solution)/shard_map/ppermute | solution.py:280
  59.9 10.9 %collective-permute-done.16.refs_2_ = bf16[8,8,2048]{2,1,0:T(8,128)(2,1)S(1)} collective-permute-done((bf16[8,8,2048]{2,1,0:T(8,128)(2,1)S(1)}, bf16[8,8,2048]{2,1,0:T(8,128)(2,1)S(1)}, u32[]{:S(2)}, u32[]{:S(2)}) %collective-permute-start.16) | collective-permute-done | bytes 262176 | tf_op jit(solution)/shard_map/ppermute | solution.py:280
  70.9 4.7 %collective-permute-start.23 = (bf16[8,8,2048]{2,1,0:T(8,128)(2,1)S(1)}, bf16[8,8,2048]{2,1,0:T(8,128)(2,1)S(1)}, u32[]{:S(2)}, u32[]{:S(2)}) collective-permute-start(bf16[8,8,2048]{2,1,0:T(8,128)(2,1)S(1)} %get-tuple-element.89), channel_id=1, source_target_pairs={{0,7},{1,6},{2,5},{3,4},{4,3},{5,2},{6,1},{7,0},{8,15},{9,14},{10,... | collective-permute-start | bytes 786440 | tf_op jit(solution)/shard_map/ppermute | solution.py:280
  76.6 6.0 %collective-permute-done.21.refs_7_ = bf16[8,8,2048]{2,1,0:T(8,128)(2,1)S(1)} collective-permute-done((bf16[8,8,2048]{2,1,0:T(8,128)(2,1)S(1)}, bf16[8,8,2048]{2,1,0:T(8,128)(2,1)S(1)}, u32[]{:S(2)}, u32[]{:S(2)}) %collective-permute-start.21) | collective-permute-done | bytes 262176 | tf_op jit(solution)/shard_map/ppermute | solution.py:280
  82.6 4.2 %collective-permute-start.27 = (bf16[8,8,2048]{2,1,0:T(8,128)(2,1)S(1)}, bf16[8,8,2048]{2,1,0:T(8,128)(2,1)S(1)}, u32[]{:S(2)}, u32[]{:S(2)}) collective-permute-start(bf16[8,8,2048]{2,1,0:T(8,128)(2,1)S(1)} %get-tuple-element.93), channel_id=1, source_target_pairs={{0,5},{1,4},{2,7},{3,6},{4,1},{5,0},{6,3},{7,2},{8,13},{9,12},{10,... | collective-permute-start | bytes 786440 | tf_op jit(solution)/shard_map/ppermute | solution.py:280
  86.9 10.2 %collective-permute-start.28 = (bf16[8,8,2048]{2,1,0:T(8,128)(2,1)S(1)}, bf16[8,8,2048]{2,1,0:T(8,128)(2,1)S(1)}, u32[]{:S(2)}, u32[]{:S(2)}) collective-permute-start(bf16[8,8,2048]{2,1,0:T(8,128)(2,1)S(1)} %get-tuple-element.94), channel_id=1, source_target_pairs={{0,13},{1,12},{2,15},{3,14},{4,9},{5,8},{6,11},{7,10},{8,5},{9,4},... | collective-permute-start | bytes 786440 | tf_op jit(solution)/shard_map/ppermute | solution.py:280
  98.1 5.8 %collective-permute-done.28.refs_14_ = bf16[8,8,2048]{2,1,0:T(8,128)(2,1)S(1)} collective-permute-done((bf16[8,8,2048]{2,1,0:T(8,128)(2,1)S(1)}, bf16[8,8,2048]{2,1,0:T(8,128)(2,1)S(1)}, u32[]{:S(2)}, u32[]{:S(2)}) %collective-permute-start.28) | collective-permute-done | bytes 262176 | tf_op jit(solution)/shard_map/ppermute | solution.py:280
  103.9 4.3 %collective-permute-start.13 = (bf16[8,8,2048]{2,1,0:T(8,128)(2,1)}, bf16[8,8,2048]{2,1,0:T(8,128)(2,1)}, u32[]{:S(2)}, u32[]{:S(2)}) collective-permute-start(bf16[8,8,2048]{2,1,0:T(8,128)(2,1)} %get-tuple-element.78), channel_id=1, source_target_pairs={{0,13},{1,12},{2,15},{3,14},{4,9},{5,8},{6,11},{7,10},{8,5},{9,4},... | collective-permute-start | bytes 786440 | tf_op jit(solution)/shard_map/ppermute | solution.py:280
  108.3 5.2 %shard_map.103 = bf16[16,2,8,8,128]{4,3,2,1,0:T(8,128)(2,1)} custom-call(s32[2]{0:T(128)S(1)} %pad_add_fusion.me_ref, bf16[8,128,2048]{2,1,0:T(8,128)(2,1)S(1)} %copy-done, bf16[8,8,2048]{2,1,0:T(8,128)(2,1)S(1)} %get-tuple-element.61.refs_0_, bf16[8,8,2048]{2,1,0:T(8,128)(2,1)S(1)} %collective-permute-done.15.refs_1_, ...), custom_call_target="tpu_custom_call" | custom-call | flops 1073741824 | bytes 8388608 | tf_op jit(solution)/shard_map/pallas_call | solution.py:260
  113.6 7.0 %all-to-all-start = ((bf16[16,2,8,8,128]{4,3,2,1,0:T(8,128)(2,1)}), bf16[16,2,8,8,128]{4,3,2,1,0:T(8,128)(2,1)S(1)}, u32[]{:S(2)}, u32[]{:S(2)}) async-start(bf16[16,2,8,8,128]{4,3,2,1,0:T(8,128)(2,1)} %shard_map.103), calls=%async_computation | async-start | bytes 1048576 | tf_op jit(solution)/shard_map/all_to_all | solution.py:378
  120.6 2.2 %copy-done.1 = bf16[8,128,2048]{2,1,0:T(8,128)(2,1)S(1)} copy-done((bf16[8,128,2048]{2,1,0:T(8,128)(2,1)S(1)}, bf16[8,128,2048]{2,1,0:T(8,128)(2,1)}, u32[]{:S(2)}) %copy-start.1) | copy-done | bytes 4194328
  122.7 2.2 %copy-done.2 = bf16[8,128,2048]{2,1,0:T(8,128)(2,1)S(1)} copy-done((bf16[8,128,2048]{2,1,0:T(8,128)(2,1)S(1)}, bf16[8,128,2048]{2,1,0:T(8,128)(2,1)}, u32[]{:S(2)}) %copy-start.2) | copy-done | bytes 4194328
  124.9 4.3 %shard_map.101 = (f32[2,4,2,8,8,128]{5,4,3,2,1,0:T(8,128)S(1)}, bf16[2,4,2,8,8,128]{5,4,3,2,1,0:T(8,128)(2,1)S(1)}) custom-call(s32[2]{0:T(128)S(1)} %pad_add_fusion.me_ref, bf16[8,128,2048]{2,1,0:T(8,128)(2,1)S(1)} %copy-done.2, bf16[8,128,2048]{2,1,0:T(8,128)(2,1)S(1)} %copy-done.1), custom_call_target="tpu_custom_call" | custom-call | flops 1073741824 | bytes 8388608 | tf_op jit(solution)/shard_map/pallas_call | solution.py:183
  129.2 3.5 %collective-permute-start.30 = (bf16[2,4,2,8,8,128]{5,4,3,2,1,0:T(8,128)(2,1)S(1)}, bf16[2,4,2,8,8,128]{5,4,3,2,1,0:T(8,128)(2,1)S(1)}, u32[]{:S(2)}, u32[]{:S(2)}) collective-permute-start(bf16[2,4,2,8,8,128]{5,4,3,2,1,0:T(8,128)(2,1)S(1)} %get-tuple-element.96), channel_id=1, source_target_pairs={{0,128},{16,144},{32,160},{48,176},{64,192},{80,208},{96,224},{112... | collective-permute-start | bytes 786440 | tf_op jit(solution)/shard_map/ppermute | solution.py:320
  132.8 8.2 %shard_map.102 = (bf16[8,128,2048]{2,1,0:T(8,128)(2,1)}, f32[2,4,2,8,8,128]{5,4,3,2,1,0:T(8,128)S(1)}, bf16[2,4,2,8,8,128]{5,4,3,2,1,0:T(8,128)(2,1)S(1)}) custom-call(s32[2]{0:T(128)S(1)} %pad_add_fusion.me_ref, bf16[8,128,128]{2,1,0:T(8,128)(2,1)S(1)} %copy-done.4, bf16[8,128,2048]{2,1,0:T(8,128)(2,1)S(1)} %copy-done.3, ...), custom_call_target="tpu_custom_call" | custom-call | flops 2147483648 | bytes 12582912 | tf_op jit(solution)/shard_map/pallas_call | solution.py:223
  141.1 9.1 %collective-permute-done.31.refs_3_ = bf16[2,4,2,8,8,128]{5,4,3,2,1,0:T(8,128)(2,1)S(1)} collective-permute-done((bf16[2,4,2,8,8,128]{5,4,3,2,1,0:T(8,128)(2,1)S(1)}, bf16[2,4,2,8,8,128]{5,4,3,2,1,0:T(8,128)(2,1)S(1)}, u32[]{:S(2)}, u32[]{:S(2)}) %collective-permute-start.31) | collective-permute-done | bytes 262176 | tf_op jit(solution)/shard_map/ppermute | solution.py:320
  151.6 6.2 %collective-permute-done.32.refs_1_ = bf16[4,4,8,8,128]{4,3,2,1,0:T(8,128)(2,1)S(1)} collective-permute-done((bf16[4,4,8,8,128]{4,3,2,1,0:T(8,128)(2,1)S(1)}, bf16[4,4,8,8,128]{4,3,2,1,0:T(8,128)(2,1)S(1)}, u32[]{:S(2)}, u32[]{:S(2)}) %collective-permute-start.32) | collective-permute-done | bytes 262176 | tf_op jit(solution)/shard_map/ppermute | solution.py:320
  158.4 5.5 %collective-permute-start.33 = (bf16[2,4,8,8,128]{4,3,2,1,0:T(8,128)(2,1)S(1)}, bf16[2,4,8,8,128]{4,3,2,1,0:T(8,128)(2,1)S(1)}, u32[]{:S(2)}, u32[]{:S(2)}) collective-permute-start(bf16[2,4,8,8,128]{4,3,2,1,0:T(8,128)(2,1)S(1)} %get-tuple-element.102), channel_id=1, source_target_pairs={{0,32},{16,48},{32,0},{48,16},{64,96},{80,112},{96,64},{112,80},{1... | collective-permute-start | bytes 393224 | tf_op jit(solution)/shard_map/ppermute | solution.py:320
  163.9 4.8 %collective-permute-done.33.refs_1_ = bf16[2,4,8,8,128]{4,3,2,1,0:T(8,128)(2,1)S(1)} collective-permute-done((bf16[2,4,8,8,128]{4,3,2,1,0:T(8,128)(2,1)S(1)}, bf16[2,4,8,8,128]{4,3,2,1,0:T(8,128)(2,1)S(1)}, u32[]{:S(2)}, u32[]{:S(2)}) %collective-permute-start.33) | collective-permute-done | bytes 131104 | tf_op jit(solution)/shard_map/ppermute | solution.py:320
  169.2 2.7 %collective-permute-start.34 = (bf16[4,8,8,128]{3,2,1,0:T(8,128)(2,1)S(1)}, bf16[4,8,8,128]{3,2,1,0:T(8,128)(2,1)S(1)}, u32[]{:S(2)}, u32[]{:S(2)}) collective-permute-start(bf16[4,8,8,128]{3,2,1,0:T(8,128)(2,1)S(1)} %get-tuple-element.104), channel_id=1, source_target_pairs={{0,16},{16,0},{32,48},{48,32},{64,80},{80,64},{96,112},{112,96},{1... | collective-permute-start | bytes 196616 | tf_op jit(solution)/shard_map/ppermute | solution.py:320
  171.9 3.3 %collective-permute-done.34.got_ref = bf16[4,8,8,128]{3,2,1,0:T(8,128)(2,1)S(1)} collective-permute-done((bf16[4,8,8,128]{3,2,1,0:T(8,128)(2,1)S(1)}, bf16[4,8,8,128]{3,2,1,0:T(8,128)(2,1)S(1)}, u32[]{:S(2)}, u32[]{:S(2)}) %collective-permute-start.34) | collective-permute-done | bytes 65568 | tf_op jit(solution)/shard_map/ppermute | solution.py:320
  (64 shorter events, 13.8 us)
Async XLA Ops:
  9.3 21.5 %collective-permute-start.1 = (bf16[8,8,2048]{2,1,0:T(8,128)(2,1)S(1)}, bf16[8,8,2048]{2,1,0:T(8,128)(2,1)S(1)}, u32[]{:S(2)}, u32[]{:S(2)}) collective-permute-start(bf16[8,8,2048]{2,1,0:T(8,128)(2,1)S(1)} %get-tuple-element.66), channel_id=1, source_target_pairs={{0,6},{1,7},{2,4},{3,5},{4,2},{5,3},{6,0},{7,1},{8,14},{9,15},{10,... | collective-permute-start | bytes 786440 | tf_op jit(solution)/shard_map/ppermute | solution.py:280
  11.5 22.9 %collective-permute-start.2 = (bf16[8,8,2048]{2,1,0:T(8,128)(2,1)S(1)}, bf16[8,8,2048]{2,1,0:T(8,128)(2,1)S(1)}, u32[]{:S(2)}, u32[]{:S(2)}) collective-permute-start(bf16[8,8,2048]{2,1,0:T(8,128)(2,1)S(1)} %get-tuple-element.67), channel_id=1, source_target_pairs={{0,14},{1,15},{2,12},{3,13},{4,10},{5,11},{6,8},{7,9},{8,6},{9,7},... | collective-permute-start | bytes 786440 | tf_op jit(solution)/shard_map/ppermute | solution.py:280
  12.6 21.8 %collective-permute-start.3 = (bf16[8,8,2048]{2,1,0:T(8,128)(2,1)S(1)}, bf16[8,8,2048]{2,1,0:T(8,128)(2,1)S(1)}, u32[]{:S(2)}, u32[]{:S(2)}) collective-permute-start(bf16[8,8,2048]{2,1,0:T(8,128)(2,1)S(1)} %get-tuple-element.68), channel_id=1, source_target_pairs={{0,2},{1,3},{2,0},{3,1},{4,6},{5,7},{6,4},{7,5},{8,10},{9,11},{10,... | collective-permute-start | bytes 786440 | tf_op jit(solution)/shard_map/ppermute | solution.py:280
  13.6 22.0 %collective-permute-start.4 = (bf16[8,8,2048]{2,1,0:T(8,128)(2,1)S(1)}, bf16[8,8,2048]{2,1,0:T(8,128)(2,1)S(1)}, u32[]{:S(2)}, u32[]{:S(2)}) collective-permute-start(bf16[8,8,2048]{2,1,0:T(8,128)(2,1)S(1)} %get-tuple-element.69), channel_id=1, source_target_pairs={{0,8},{1,9},{2,10},{3,11},{4,12},{5,13},{6,14},{7,15},{8,0},{9,1},... | collective-permute-start | bytes 786440 | tf_op jit(solution)/shard_map/ppermute | solution.py:280
  17.6 24.0 %collective-permute-start.5 = (bf16[8,8,2048]{2,1,0:T(8,128)(2,1)S(1)}, bf16[8,8,2048]{2,1,0:T(8,128)(2,1)S(1)}, u32[]{:S(2)}, u32[]{:S(2)}) collective-permute-start(bf16[8,8,2048]{2,1,0:T(8,128)(2,1)S(1)} %get-tuple-element.70), channel_id=1, source_target_pairs={{0,4},{1,5},{2,6},{3,7},{4,0},{5,1},{6,2},{7,3},{8,12},{9,13},{10,... | collective-permute-start | bytes 786440 | tf_op jit(solution)/shard_map/ppermute | solution.py:280
  30.9 14.9 %collective-permute-start.6 = (bf16[8,8,2048]{2,1,0:T(8,128)(2,1)S(1)}, bf16[8,8,2048]{2,1,0:T(8,128)(2,1)S(1)}, u32[]{:S(2)}, u32[]{:S(2)}) collective-permute-start(bf16[8,8,2048]{2,1,0:T(8,128)(2,1)S(1)} %get-tuple-element.71), channel_id=1, source_target_pairs={{0,12},{1,13},{2,14},{3,15},{4,8},{5,9},{6,10},{7,11},{8,4},{9,5},... | collective-permute-start | bytes 786440 | tf_op jit(solution)/shard_map/ppermute | solution.py:280
  34.4 11.5 %collective-permute-start.7 = (bf16[8,8,2048]{2,1,0:T(8,128)(2,1)S(1)}, bf16[8,8,2048]{2,1,0:T(8,128)(2,1)S(1)}, u32[]{:S(2)}, u32[]{:S(2)}) collective-permute-start(bf16[8,8,2048]{2,1,0:T(8,128)(2,1)S(1)} %get-tuple-element.72), channel_id=1, source_target_pairs={{0,11},{1,10},{2,9},{3,8},{4,15},{5,14},{6,13},{7,12},{8,3},{9,2},... | collective-permute-start | bytes 786440 | tf_op jit(solution)/shard_map/ppermute | solution.py:280
  34.4 16.2 %collective-permute-start.8 = (bf16[8,8,2048]{2,1,0:T(8,128)(2,1)S(1)}, bf16[8,8,2048]{2,1,0:T(8,128)(2,1)S(1)}, u32[]{:S(2)}, u32[]{:S(2)}) collective-permute-start(bf16[8,8,2048]{2,1,0:T(8,128)(2,1)S(1)} %get-tuple-element.73), channel_id=1, source_target_pairs={{0,7},{1,6},{2,5},{3,4},{4,3},{5,2},{6,1},{7,0},{8,15},{9,14},{10,... | collective-permute-start | bytes 786440 | tf_op jit(solution)/shard_map/ppermute | solution.py:280
  35.6 18.3 %collective-permute-start.9 = (bf16[8,8,2048]{2,1,0:T(8,128)(2,1)S(1)}, bf16[8,8,2048]{2,1,0:T(8,128)(2,1)S(1)}, u32[]{:S(2)}, u32[]{:S(2)}) collective-permute-start(bf16[8,8,2048]{2,1,0:T(8,128)(2,1)S(1)} %get-tuple-element.74), channel_id=1, source_target_pairs={{0,15},{1,14},{2,13},{3,12},{4,11},{5,10},{6,9},{7,8},{8,7},{9,6},... | collective-permute-start | bytes 786440 | tf_op jit(solution)/shard_map/ppermute | solution.py:280
  41.6 18.3 %collective-permute-start.15 = (bf16[8,8,2048]{2,1,0:T(8,128)(2,1)S(1)}, bf16[8,8,2048]{2,1,0:T(8,128)(2,1)S(1)}, u32[]{:S(2)}, u32[]{:S(2)}) collective-permute-start(bf16[8,8,2048]{2,1,0:T(8,128)(2,1)S(1)} %get-tuple-element.81), channel_id=1, source_target_pairs={{0,10},{1,11},{2,8},{3,9},{4,14},{5,15},{6,12},{7,13},{8,2},{9,3},... | collective-permute-start | bytes 786440 | tf_op jit(solution)/shard_map/ppermute | solution.py:280
  45.8 25.1 %collective-permute-start.16 = (bf16[8,8,2048]{2,1,0:T(8,128)(2,1)S(1)}, bf16[8,8,2048]{2,1,0:T(8,128)(2,1)S(1)}, u32[]{:S(2)}, u32[]{:S(2)}) collective-permute-start(bf16[8,8,2048]{2,1,0:T(8,128)(2,1)S(1)} %get-tuple-element.82), channel_id=1, source_target_pairs={{0,6},{1,7},{2,4},{3,5},{4,2},{5,3},{6,0},{7,1},{8,14},{9,15},{10,... | collective-permute-start | bytes 786440 | tf_op jit(solution)/shard_map/ppermute | solution.py:280
  45.9 25.0 %collective-permute-start.17 = (bf16[8,8,2048]{2,1,0:T(8,128)(2,1)S(1)}, bf16[8,8,2048]{2,1,0:T(8,128)(2,1)S(1)}, u32[]{:S(2)}, u32[]{:S(2)}) collective-permute-start(bf16[8,8,2048]{2,1,0:T(8,128)(2,1)S(1)} %get-tuple-element.83), channel_id=1, source_target_pairs={{0,14},{1,15},{2,12},{3,13},{4,10},{5,11},{6,8},{7,9},{8,6},{9,7},... | collective-permute-start | bytes 786440 | tf_op jit(solution)/shard_map/ppermute | solution.py:280
  50.5 20.3 %collective-permute-start.18 = (bf16[8,8,2048]{2,1,0:T(8,128)(2,1)S(1)}, bf16[8,8,2048]{2,1,0:T(8,128)(2,1)S(1)}, u32[]{:S(2)}, u32[]{:S(2)}) collective-permute-start(bf16[8,8,2048]{2,1,0:T(8,128)(2,1)S(1)} %get-tuple-element.84), channel_id=1, source_target_pairs={{0,2},{1,3},{2,0},{3,1},{4,6},{5,7},{6,4},{7,5},{8,10},{9,11},{10,... | collective-permute-start | bytes 786440 | tf_op jit(solution)/shard_map/ppermute | solution.py:280
  54.6 21.0 %collective-permute-start.19 = (bf16[8,8,2048]{2,1,0:T(8,128)(2,1)S(1)}, bf16[8,8,2048]{2,1,0:T(8,128)(2,1)S(1)}, u32[]{:S(2)}, u32[]{:S(2)}) collective-permute-start(bf16[8,8,2048]{2,1,0:T(8,128)(2,1)S(1)} %get-tuple-element.85), channel_id=1, source_target_pairs={{0,8},{1,9},{2,10},{3,11},{4,12},{5,13},{6,14},{7,15},{8,0},{9,1},... | collective-permute-start | bytes 786440 | tf_op jit(solution)/shard_map/ppermute | solution.py:280
  59.9 15.7 %collective-permute-start.20 = (bf16[8,8,2048]{2,1,0:T(8,128)(2,1)S(1)}, bf16[8,8,2048]{2,1,0:T(8,128)(2,1)S(1)}, u32[]{:S(2)}, u32[]{:S(2)}) collective-permute-start(bf16[8,8,2048]{2,1,0:T(8,128)(2,1)S(1)} %get-tuple-element.86), channel_id=1, source_target_pairs={{0,4},{1,5},{2,6},{3,7},{4,0},{5,1},{6,2},{7,3},{8,12},{9,13},{10,... | collective-permute-start | bytes 786440 | tf_op jit(solution)/shard_map/ppermute | solution.py:280
  70.8 11.7 %collective-permute-start.21 = (bf16[8,8,2048]{2,1,0:T(8,128)(2,1)S(1)}, bf16[8,8,2048]{2,1,0:T(8,128)(2,1)S(1)}, u32[]{:S(2)}, u32[]{:S(2)}) collective-permute-start(bf16[8,8,2048]{2,1,0:T(8,128)(2,1)S(1)} %get-tuple-element.87), channel_id=1, source_target_pairs={{0,12},{1,13},{2,14},{3,15},{4,8},{5,9},{6,10},{7,11},{8,4},{9,5},... | collective-permute-start | bytes 786440 | tf_op jit(solution)/shard_map/ppermute | solution.py:280
  70.9 11.8 %collective-permute-start.22 = (bf16[8,8,2048]{2,1,0:T(8,128)(2,1)S(1)}, bf16[8,8,2048]{2,1,0:T(8,128)(2,1)S(1)}, u32[]{:S(2)}, u32[]{:S(2)}) collective-permute-start(bf16[8,8,2048]{2,1,0:T(8,128)(2,1)S(1)} %get-tuple-element.88), channel_id=1, source_target_pairs={{0,11},{1,10},{2,9},{3,8},{4,15},{5,14},{6,13},{7,12},{8,3},{9,2},... | collective-permute-start | bytes 786440 | tf_op jit(solution)/shard_map/ppermute | solution.py:280
  70.9 16.0 %collective-permute-start.23 = (bf16[8,8,2048]{2,1,0:T(8,128)(2,1)S(1)}, bf16[8,8,2048]{2,1,0:T(8,128)(2,1)S(1)}, u32[]{:S(2)}, u32[]{:S(2)}) collective-permute-start(bf16[8,8,2048]{2,1,0:T(8,128)(2,1)S(1)} %get-tuple-element.89), channel_id=1, source_target_pairs={{0,7},{1,6},{2,5},{3,4},{4,3},{5,2},{6,1},{7,0},{8,15},{9,14},{10,... | collective-permute-start | bytes 786440 | tf_op jit(solution)/shard_map/ppermute | solution.py:280
  75.6 21.6 %collective-permute-start.24 = (bf16[8,8,2048]{2,1,0:T(8,128)(2,1)S(1)}, bf16[8,8,2048]{2,1,0:T(8,128)(2,1)S(1)}, u32[]{:S(2)}, u32[]{:S(2)}) collective-permute-start(bf16[8,8,2048]{2,1,0:T(8,128)(2,1)S(1)} %get-tuple-element.90), channel_id=1, source_target_pairs={{0,15},{1,14},{2,13},{3,12},{4,11},{5,10},{6,9},{7,8},{8,7},{9,6},... | collective-permute-start | bytes 786440 | tf_op jit(solution)/shard_map/ppermute | solution.py:280
  75.6 21.9 %collective-permute-start.25 = (bf16[8,8,2048]{2,1,0:T(8,128)(2,1)S(1)}, bf16[8,8,2048]{2,1,0:T(8,128)(2,1)S(1)}, u32[]{:S(2)}, u32[]{:S(2)}) collective-permute-start(bf16[8,8,2048]{2,1,0:T(8,128)(2,1)S(1)} %get-tuple-element.91), channel_id=1, source_target_pairs={{0,3},{1,2},{2,1},{3,0},{4,7},{5,6},{6,5},{7,4},{8,11},{9,10},{10,... | collective-permute-start | bytes 786440 | tf_op jit(solution)/shard_map/ppermute | solution.py:280
  82.6 15.0 %collective-permute-start.26 = (bf16[8,8,2048]{2,1,0:T(8,128)(2,1)S(1)}, bf16[8,8,2048]{2,1,0:T(8,128)(2,1)S(1)}, u32[]{:S(2)}, u32[]{:S(2)}) collective-permute-start(bf16[8,8,2048]{2,1,0:T(8,128)(2,1)S(1)} %get-tuple-element.92), channel_id=1, source_target_pairs={{0,9},{1,8},{2,11},{3,10},{4,13},{5,12},{6,15},{7,14},{8,1},{9,0},... | collective-permute-start | bytes 786440 | tf_op jit(solution)/shard_map/ppermute | solution.py:280
  82.6 15.0 %collective-permute-start.27 = (bf16[8,8,2048]{2,1,0:T(8,128)(2,1)S(1)}, bf16[8,8,2048]{2,1,0:T(8,128)(2,1)S(1)}, u32[]{:S(2)}, u32[]{:S(2)}) collective-permute-start(bf16[8,8,2048]{2,1,0:T(8,128)(2,1)S(1)} %get-tuple-element.93), channel_id=1, source_target_pairs={{0,5},{1,4},{2,7},{3,6},{4,1},{5,0},{6,3},{7,2},{8,13},{9,12},{10,... | collective-permute-start | bytes 786440 | tf_op jit(solution)/shard_map/ppermute | solution.py:280
  86.9 17.0 %collective-permute-start.28 = (bf16[8,8,2048]{2,1,0:T(8,128)(2,1)S(1)}, bf16[8,8,2048]{2,1,0:T(8,128)(2,1)S(1)}, u32[]{:S(2)}, u32[]{:S(2)}) collective-permute-start(bf16[8,8,2048]{2,1,0:T(8,128)(2,1)S(1)} %get-tuple-element.94), channel_id=1, source_target_pairs={{0,13},{1,12},{2,15},{3,14},{4,9},{5,8},{6,11},{7,10},{8,5},{9,4},... | collective-permute-start | bytes 786440 | tf_op jit(solution)/shard_map/ppermute | solution.py:280
  97.1 11.1 %collective-permute-start.29 = (bf16[8,8,2048]{2,1,0:T(8,128)(2,1)S(1)}, bf16[8,8,2048]{2,1,0:T(8,128)(2,1)S(1)}, u32[]{:S(2)}, u32[]{:S(2)}) collective-permute-start(bf16[8,8,2048]{2,1,0:T(8,128)(2,1)S(1)} %get-tuple-element.95), channel_id=1, source_target_pairs={{0,1},{1,0},{2,3},{3,2},{4,5},{5,4},{6,7},{7,6},{8,9},{9,8},{10,11... | collective-permute-start | bytes 786440 | tf_op jit(solution)/shard_map/ppermute | solution.py:280
  97.5 31.7 %collective-permute-start.10 = (bf16[8,8,2048]{2,1,0:T(8,128)(2,1)}, bf16[8,8,2048]{2,1,0:T(8,128)(2,1)}, u32[]{:S(2)}, u32[]{:S(2)}) collective-permute-start(bf16[8,8,2048]{2,1,0:T(8,128)(2,1)} %get-tuple-element.75), channel_id=1, source_target_pairs={{0,3},{1,2},{2,1},{3,0},{4,7},{5,6},{6,5},{7,4},{8,11},{9,10},{10,... | collective-permute-start | bytes 786440 | tf_op jit(solution)/shard_map/ppermute | solution.py:280
  97.5 35.2 %collective-permute-start.11 = (bf16[8,8,2048]{2,1,0:T(8,128)(2,1)}, bf16[8,8,2048]{2,1,0:T(8,128)(2,1)}, u32[]{:S(2)}, u32[]{:S(2)}) collective-permute-start(bf16[8,8,2048]{2,1,0:T(8,128)(2,1)} %get-tuple-element.76), channel_id=1, source_target_pairs={{0,9},{1,8},{2,11},{3,10},{4,13},{5,12},{6,15},{7,14},{8,1},{9,0},... | collective-permute-start | bytes 786440 | tf_op jit(solution)/shard_map/ppermute | solution.py:280
  97.7 35.1 %collective-permute-start.12 = (bf16[8,8,2048]{2,1,0:T(8,128)(2,1)}, bf16[8,8,2048]{2,1,0:T(8,128)(2,1)}, u32[]{:S(2)}, u32[]{:S(2)}) collective-permute-start(bf16[8,8,2048]{2,1,0:T(8,128)(2,1)} %get-tuple-element.77), channel_id=1, source_target_pairs={{0,5},{1,4},{2,7},{3,6},{4,1},{5,0},{6,3},{7,2},{8,13},{9,12},{10,... | collective-permute-start | bytes 786440 | tf_op jit(solution)/shard_map/ppermute | solution.py:280
  103.9 28.9 %collective-permute-start.13 = (bf16[8,8,2048]{2,1,0:T(8,128)(2,1)}, bf16[8,8,2048]{2,1,0:T(8,128)(2,1)}, u32[]{:S(2)}, u32[]{:S(2)}) collective-permute-start(bf16[8,8,2048]{2,1,0:T(8,128)(2,1)} %get-tuple-element.78), channel_id=1, source_target_pairs={{0,13},{1,12},{2,15},{3,14},{4,9},{5,8},{6,11},{7,10},{8,5},{9,4},... | collective-permute-start | bytes 786440 | tf_op jit(solution)/shard_map/ppermute | solution.py:280
  108.2 24.6 %collective-permute-start.14 = (bf16[8,8,2048]{2,1,0:T(8,128)(2,1)}, bf16[8,8,2048]{2,1,0:T(8,128)(2,1)}, u32[]{:S(2)}, u32[]{:S(2)}) collective-permute-start(bf16[8,8,2048]{2,1,0:T(8,128)(2,1)} %get-tuple-element.79), channel_id=1, source_target_pairs={{0,1},{1,0},{2,3},{3,2},{4,5},{5,4},{6,7},{7,6},{8,9},{9,8},{10,11... | collective-permute-start | bytes 786440 | tf_op jit(solution)/shard_map/ppermute | solution.py:280
  113.6 61.6 %all-to-all-start = ((bf16[16,2,8,8,128]{4,3,2,1,0:T(8,128)(2,1)}), bf16[16,2,8,8,128]{4,3,2,1,0:T(8,128)(2,1)S(1)}, u32[]{:S(2)}, u32[]{:S(2)}) async-start(bf16[16,2,8,8,128]{4,3,2,1,0:T(8,128)(2,1)} %shard_map.103), calls=%async_computation | async-start | bytes 1048576 | tf_op jit(solution)/shard_map/all_to_all | solution.py:378
  129.2 11.8 %collective-permute-start.30 = (bf16[2,4,2,8,8,128]{5,4,3,2,1,0:T(8,128)(2,1)S(1)}, bf16[2,4,2,8,8,128]{5,4,3,2,1,0:T(8,128)(2,1)S(1)}, u32[]{:S(2)}, u32[]{:S(2)}) collective-permute-start(bf16[2,4,2,8,8,128]{5,4,3,2,1,0:T(8,128)(2,1)S(1)} %get-tuple-element.96), channel_id=1, source_target_pairs={{0,128},{16,144},{32,160},{48,176},{64,192},{80,208},{96,224},{112... | collective-permute-start | bytes 786440 | tf_op jit(solution)/shard_map/ppermute | solution.py:320
  158.4 10.2 %collective-permute-start.33 = (bf16[2,4,8,8,128]{4,3,2,1,0:T(8,128)(2,1)S(1)}, bf16[2,4,8,8,128]{4,3,2,1,0:T(8,128)(2,1)S(1)}, u32[]{:S(2)}, u32[]{:S(2)}) collective-permute-start(bf16[2,4,8,8,128]{4,3,2,1,0:T(8,128)(2,1)S(1)} %get-tuple-element.102), channel_id=1, source_target_pairs={{0,32},{16,48},{32,0},{48,16},{64,96},{80,112},{96,64},{112,80},{1... | collective-permute-start | bytes 393224 | tf_op jit(solution)/shard_map/ppermute | solution.py:320
  (11 other events, 195.6 us)

commit v2 on v1

--- a/solution.py
+++ b/solution.py
@@ -96,8 +96,7 @@
     return jnp.dot(p, v.reshape(a * b, t), preferred_element_type=F32)
 
 
-def send_h_kernel(n, me_ref, w_ref, x_hbm, *refs):
-    outs, (xbuf, wbuf, wt, hid, sems) = refs[:n], refs[n:]
+def send_h_kernel(n, me_ref, w_ref, x_hbm, own_ref, other_ref, xbuf, wbuf, wt, hid, sems):
     nb, bs, _ = w_ref.shape
     rows = bs // n
     me = me_ref[0]
@@ -117,8 +116,9 @@
     p = swap_matrix(rows)
     for k in range(n):
         s = swap(p, hid[k])
+        o_ref = other_ref if k % 2 else own_ref
         for j in range(rows):
-            outs[k][j] = s[j * nb : (j + 1) * nb].astype(BF)
+            o_ref[k // 2, j] = s[j * nb : (j + 1) * nb].astype(BF)
 
 
 def send_h(me, w_first, layer_input, n):
@@ -131,8 +131,8 @@
             pl.BlockSpec(memory_space=VMEM),
             pl.BlockSpec(memory_space=pltpu.HBM),
         ],
-        out_specs=[pl.BlockSpec(memory_space=VMEM)] * n,
-        out_shape=[pltpu.VMEM((rows, nb, t), BF)] * n,
+        out_specs=[pl.BlockSpec(memory_space=VMEM)] * 2,
+        out_shape=[pltpu.VMEM((n // 2, rows, nb, t), BF)] * 2,
         scratch_shapes=[
             pltpu.VMEM((nb, bs, t), BF),
             pltpu.VMEM((n, rows, bs), BF),
@@ -145,18 +145,43 @@
     )(me, w_first, in_hbm(layer_input))
 
 
+def pack_kernel(own_ref, got_ref, *o_refs):
+    chips = own_ref.shape[0]
+    rows = o_refs[0].shape[1]
+    for part in range(PARTS):
+        for q in range(chips):
+            o_ref = o_refs[part * chips + q]
+            o_ref[0] = own_ref[q, part * rows : (part + 1) * rows]
+            o_ref[1] = got_ref[q, part * rows : (part + 1) * rows]
+
+
+def pack(own, got):
+    chips, rows, nb, t = own.shape
+    out = pltpu.VMEM((2, rows // PARTS, nb, t), BF)
+    return pl.pallas_call(
+        pack_kernel,
+        in_specs=[pl.BlockSpec(memory_space=VMEM)] * 2,
+        out_specs=[pl.BlockSpec(memory_space=VMEM)] * (PARTS * chips),
+        out_shape=[out] * (PARTS * chips),
+        compiler_params=params(4),
+        cost_estimate=cost(own.size, 8 * own.size),
+    )(own, got)
+
+
 NY = 4
 ORDER = (10, 6, 14, 2, 8, 4, 12, 11, 7, 15, 3, 9, 5, 13, 1)
 ISSUE = (0,) + ORDER
-
-
-def put(o_refs, buf, me_ref, which, b, value):
+CHIPS = (0, 5, 3, 7, 1, 4, 2, 6)
+PARTS = 2
+
+
+def put(o_refs, buf, me_ref, b, value):
     keep, send = o_refs
-    half, nh, _, _, rows, bs = keep.shape
+    half, nh, _, rows, bs = keep.shape
     buf[...] = value.reshape(2, half, nh, rows, bs)
     high = lax.div(me_ref[1], half * nh)
-    keep[:, :, which, b] = buf[high]
-    send[:, :, which, b] = buf[1 - high].astype(BF)
+    keep[:, :, b] = buf[high]
+    send[:, :, b] = buf[1 - high].astype(BF)
 
 
 def local_stats_kernel(scale, me_ref, x_ref, c_ref, *refs):
@@ -164,21 +189,21 @@
     b = pl.program_id(0)
     x = x_ref[0]
     c = c_ref[0]
-    put(o_refs, buf, me_ref, 0, b, lax.dot_general(x, x, NT, preferred_element_type=F32) * scale)
-    put(o_refs, buf, me_ref, 1, b, lax.dot_general(c, c, NT, preferred_element_type=F32) * scale)
-
-
-def pieces_of(nb, bs, d):
+    put(o_refs, buf, me_ref, b, lax.dot_general(x, x, NT, preferred_element_type=F32) * scale)
+    put(o_refs, buf, me_ref, pl.num_programs(0) + b, lax.dot_general(c, c, NT, preferred_element_type=F32) * scale)
+
+
+def pieces_of(blocks, bs, d):
     nh = d // NY
-    shape = (NY // 2, nh, 2, nb, bs // d, bs)
-    spec = pl.BlockSpec(shape, lambda b: (0, 0, 0, 0, 0, 0))
+    shape = (NY // 2, nh, blocks, bs // d, bs)
+    spec = pl.BlockSpec(shape, lambda b: (0, 0, 0, 0, 0))
     buf = pltpu.VMEM((2, NY // 2, nh, bs // d, bs), F32)
     return [spec] * 2, [jax.ShapeDtypeStruct(shape, F32), jax.ShapeDtypeStruct(shape, BF)], buf
 
 
 def local_stats(me, layer_input, cotangent, scale, d):
     nb, bs, t = layer_input.shape
-    out_specs, out_shape, buf = pieces_of(nb, bs, d)
+    out_specs, out_shape, buf = pieces_of(2 * nb, bs, d)
     spec = pl.BlockSpec((1, bs, t), lambda b: (b, 0, 0))
     return pl.pallas_call(
         functools.partial(local_stats_kernel, scale),
@@ -192,7 +217,7 @@
     )(me, layer_input, cotangent)
 
 
-def first_kernel(scale, root, n, me_ref, w_ref, x_ref, *refs):
+def first_kernel(scale, root, n, me_ref, w_ref, x_ref, keep_in, send_in, *refs):
     got = [refs[ISSUE.index(k)] for k in range(n)]
     gi_ref, o_refs, (grad, buf) = refs[n], refs[n + 1 : n + 3], refs[n + 3 :]
     nb = got[0].shape[1]
@@ -202,6 +227,9 @@
 
     @pl.when(i == 0)
     def _():
+        keep, send = o_refs
+        keep[:, :, : keep_in.shape[2]] = keep_in[...]
+        send[:, :, : send_in.shape[2]] = send_in[...]
         p = swap_matrix(rows)
         for k in range(n):
             s = swap(p, got[k][...])
@@ -212,14 +240,14 @@
     g = g.reshape(g.shape[0] * g.shape[1], g.shape[2])
     x = x_ref[0]
     gi_ref[0] = jnp.dot(w_ref[0], g, preferred_element_type=F32).astype(BF)
-    put(o_refs, buf, me_ref, 0, i, lax.dot_general(x, g, NT, preferred_element_type=F32) * root)
-    put(o_refs, buf, me_ref, 1, i, lax.dot_general(g, g, NT, preferred_element_type=F32) * scale)
-
-
-def first_block(me, w_first, layer_input, got, scale, root, d):
+    put(o_refs, buf, me_ref, 2 * nb + i, lax.dot_general(x, g, NT, preferred_element_type=F32) * root)
+    put(o_refs, buf, me_ref, 3 * nb + i, lax.dot_general(g, g, NT, preferred_element_type=F32) * scale)
+
+
+def first_block(me, w_first, layer_input, local, got, scale, root, d):
     n = len(got)
     nb, bs, t = layer_input.shape
-    out_specs, out_shape, buf = pieces_of(nb, bs, d)
+    out_specs, out_shape, buf = pieces_of(4 * nb, bs, d)
     return pl.pallas_call(
         functools.partial(first_kernel, scale, root, n),
         grid=(nb,),
@@ -228,68 +256,76 @@
             pl.BlockSpec((1, bs, bs), lambda i: (i, 0, 0)),
             pl.BlockSpec((1, bs, t), lambda i: (i, 0, 0)),
         ]
-        + [pl.BlockSpec(memory_space=VMEM)] * n,
+        + [pl.BlockSpec(memory_space=VMEM)] * (2 + n),
         out_specs=[pl.BlockSpec((1, bs, t), lambda i: (i, 0, 0))] + out_specs,
         out_shape=[jax.ShapeDtypeStruct((nb, bs, t), BF)] + out_shape,
         scratch_shapes=[pltpu.VMEM((nb, n, bs // n, t), BF), buf],
         compiler_params=params(16),
         cost_estimate=cost(8 * nb * bs * bs * t, 6 * nb * bs * t),
-    )(me, w_first, layer_input, *[got[k] for k in ISSUE])
+    )(me, w_first, layer_input, *local, *[got[k] for k in ISSUE])
 
 
 def second_kernel(scale, root, n, me_ref, c_ref, *refs):
-    got = [refs[ISSUE.index(k)] for k in range(n)]
-    o_ref, mixed = refs[n:]
+    chips = n // 2
+    got = [refs[CHIPS.index(q)] for q in range(chips)]
+    *o_refs, mixed = refs[chips:]
     me = me_ref[0]
     j = pl.program_id(0)
     for k in range(n):
-        mixed[me ^ k] = got[k][j]
+        mixed[me ^ k] = got[k // 2][k % 2, j]
     m = mixed[...]
     m = m.reshape(m.shape[0] * m.shape[1], m.shape[2])
-    d, _, _, rows, bs = o_ref.shape
     cov = lax.dot_general(m, m, NT, preferred_element_type=F32) * scale
     grad = lax.dot_general(m, c_ref[0], NT, preferred_element_type=F32) * root
-    o_ref[:, 0, j] = cov.reshape(d, rows, bs).astype(BF)
-    o_ref[:, 1, j] = grad.reshape(d, rows, bs).astype(BF)
-
-
-def second_block(me, cotangent, got, scale, root, d):
-    n = len(got)
+    if len(o_refs) == 1:
+        d, _, _, rows, bs = o_refs[0].shape
+        o_refs[0][:, 0, j] = cov.reshape(d, rows, bs).astype(BF)
+        o_refs[0][:, 1, j] = grad.reshape(d, rows, bs).astype(BF)
+    else:
+        put(o_refs[:2], o_refs[2], me_ref, j, cov)
+        put(o_refs[:2], o_refs[2], me_ref, pl.num_programs(0) + j, grad)
+
+
+def second_block(me, cotangent, got, part, scale, root, d):
+    n = 2 * len(got)
     nb, bs, t = cotangent.shape
-    shape = (d, 2, nb, bs // d, bs)
+    count = nb // PARTS
+    start = part * count
+    scratch = [pltpu.VMEM((n, bs // n, t), BF)]
+    if part < PARTS - 1:
+        out_specs, out_shape, buf = pieces_of(2 * count, bs, d)
+        scratch = [buf] + scratch
+    else:
+        shape = (d, 2, count, bs // d, bs)
+        out_specs = [pl.BlockSpec(shape, lambda j: (0, 0, 0, 0, 0))]
+        out_shape = [jax.ShapeDtypeStruct(shape, BF)]
     return pl.pallas_call(
         functools.partial(second_kernel, scale, root, n),
-        grid=(nb,),
+        grid=(count,),
         in_specs=[
             pl.BlockSpec(memory_space=SMEM),
-            pl.BlockSpec((1, bs, t), lambda j: (j, 0, 0)),
+            pl.BlockSpec((1, bs, t), lambda j: (start + j, 0, 0)),
         ]
-        + [pl.BlockSpec(memory_space=VMEM)] * n,
-        out_specs=pl.BlockSpec(shape, lambda j: (0, 0, 0, 0, 0)),
-        out_shape=jax.ShapeDtypeStruct(shape, BF),
-        scratch_shapes=[pltpu.VMEM((n, bs // n, t), BF)],
+        + [pl.BlockSpec(memory_space=VMEM)] * len(got),
+        out_specs=out_specs,
+        out_shape=out_shape,
+        scratch_shapes=scratch,
         compiler_params=params(8),
-        cost_estimate=cost(4 * nb * bs * bs * t, 4 * nb * bs * t),
-    )(me, cotangent, *[got[k] for k in ISSUE])
-
-
-def exchange(pieces):
-    n = len(pieces)
-    got = list(pieces)
-    for k in ORDER:
-        got[k] = lax.ppermute(pieces[k], "block", [(p, p ^ k) for p in range(n)])
-    return [pltpu.with_memory_space_constraint(v, pltpu.VMEM) for v in got]
+        cost_estimate=cost(4 * count * bs * bs * t, 4 * count * bs * t),
+    )(me, cotangent, *[got[q] for q in CHIPS])
 
 
 def halve_kernel(bit, sets, me_ref, *refs):
     keep, send, buf = refs[2 * sets :]
-    width = buf.shape[-4] // sets
+    at = 0
     for s in range(sets):
         total = refs[2 * s][...] + refs[2 * s + 1][...].astype(F32)
+        width = total.shape[-3]
         if sets == 1:
             buf[...] = total.reshape(buf.shape)
         else:
-            buf[:, :, s * width : (s + 1) * width] = total
+            buf[:, :, at : at + width] = total
+        at += width
     mine = lax.rem(lax.div(me_ref[1], bit), 2)
     keep[...] = buf[mine]
     send[...] = buf[1 - mine].astype(BF)
@@ -297,11 +333,9 @@
 
 def halve(me, bit, *sets):
     shape = list(sets[0][0].shape)
-    shape[-4] *= len(sets)
+    shape[-3] = sum(pair[0].shape[-3] for pair in sets)
     if shape[0] != 2:
         shape = [2, shape[0] // 2] + shape[1:]
-    elif len(shape) == 5:
-        shape = [2] + shape[1:]
     out = tuple(shape[1:])
     flat = [v for pair in sets for v in pair]
     return pl.pallas_call(
@@ -324,28 +358,47 @@
     total = v_ref[0].astype(F32)
     for k in range(1, v_ref.shape[0]):
         total = total + v_ref[k].astype(F32)
-    for s in range(total.shape[0]):
-        o_refs[s][...] = total[s]
     rest = keep_ref[...] + got_ref[...].astype(F32)
-    for s in range(rest.shape[0]):
-        o_refs[total.shape[0] + s][...] = rest[s]
-
-
-def finish(v, keep, got):
-    shape = v.shape[2:]
-    outs = v.shape[1] + keep.shape[0]
+    whole, split = o_refs[:4], o_refs[4:]
+    nb = whole[0].shape[0]
+    for s, o_ref in enumerate(whole):
+        o_ref[...] = rest[s * nb : (s + 1) * nb]
+    count = total.shape[1]
+    for s, o_ref in enumerate(split):
+        at = len(whole) * nb + s * (nb - count)
+        o_ref[: nb - count] = rest[at : at + nb - count]
+        o_ref[nb - count :] = total[s]
+
+
+def finish(v, keep, got, nb):
+    shape = (nb,) + keep.shape[1:]
     return pl.pallas_call(
         finish_kernel,
         in_specs=[pl.BlockSpec(memory_space=VMEM)] * 3,
-        out_specs=[pl.BlockSpec(memory_space=VMEM)] * outs,
-        out_shape=[jax.ShapeDtypeStruct(shape, F32)] * outs,
+        out_specs=[pl.BlockSpec(memory_space=VMEM)] * 6,
+        out_shape=[jax.ShapeDtypeStruct(shape, F32)] * 6,
         compiler_params=params(6),
         cost_estimate=cost(2 * v.size, 6 * v.size),
     )(v, keep, got)
 
 
+def swap_block(v, k):
+    n = lax.axis_size("block")
+    return lax.ppermute(v, "block", [(p, p ^ k) for p in range(n)])
+
+
+def exchange(pieces):
+    got = [pieces[0]] + [swap_block(pieces[k], k) for k in range(1, len(pieces))]
+    return [pltpu.with_memory_space_constraint(v, pltpu.VMEM) for v in got]
+
+
+def exchange_chips(pieces):
+    got = [pieces[0]] + [swap_block(pieces[q], 2 * q) for q in range(1, len(pieces))]
+    return [pltpu.with_memory_space_constraint(v, pltpu.VMEM) for v in got]
+
+
 def per_device(layer_input, w_first, w_second, cotangent):
-    _, _, t = layer_input.shape
+    nb, _, t = layer_input.shape
     n = lax.axis_size("block")
     d = lax.axis_size("dp")
     total = t * d
@@ -361,22 +414,28 @@
 
     out_g = send_g(me, w_second, cotangent, n)
     got_g = exchange(out_g)
-    out_h = send_h(me, w_first, after(layer_input, out_g[0]), n)
-    got_h = exchange(out_h)
-    local = local_stats(me, after(layer_input, out_h[0]), cotangent, scale, d)
-    local_got = swap_dp(local[1], d // 2)
-    x3 = after(layer_input, local[0])
-    grad_input, *first = first_block(me, w_first, x3, got_g, scale, root, d)
+    own, other = send_h(me, w_first, after(layer_input, out_g[0]), n)
+    other = swap_block(other, 1)
+    local = local_stats(me, after(layer_input, own), cotangent, scale, d)
+    packed = pack(own, pltpu.with_memory_space_constraint(other, pltpu.VMEM))
+    got_h1 = exchange_chips(packed[: n // 2])
+    got_h2 = exchange_chips(packed[n // 2 :])
+    x3 = after(layer_input, packed[0])
+    grad_input, *first = first_block(me, w_first, x3, local, got_g, scale, root, d)
     first_got = swap_dp(first[1], d // 2)
-    keep, send = halve(me, d // 4, (local[0], local_got), (first[0], first_got))
+    c2 = after(cotangent, first[0])
+    half = second_block(me, c2, got_h1, 0, scale, root, d)
+    half_got = swap_dp(half[1], d // 2)
+    keep, send = halve(me, d // 4, (first[0], first_got), (half[0], half_got))
     got = swap_dp(send, d // 4)
     keep, send = halve(me, d // 8, (keep, got))
     got = swap_dp(send, d // 8)
-    second = second_block(me, cotangent, got_h, scale, root, d)
+    c3 = after(cotangent, half[0])
+    (second,) = second_block(me, c3, got_h2, 1, scale, root, d)
     keep, send = halve(me, d // 16, (keep, got))
     got = swap_dp(send, d // 16)
     second = lax.all_to_all(second, "dp", 0, 0, tiled=True)
-    cov2, grad2, cov_in1, cov_out2, grad1, cov_out1 = finish(second, keep, got)
+    cov_in1, cov_out2, grad1, cov_out1, cov2, grad2 = finish(second, keep, got, nb)
     return (grad_input, grad1, grad2, cov_in1, cov_out1, cov2, cov_out2)
 
 

time: 176 us -> 175 us (level)
  the two profiles are of different devices: /device:TPU:2 before, /device:TPU:8 now
where the time goes in v2:
time: 175 us
  waiting for transfers between devices  79 us (45%)
  starting transfers between devices  63.2 us (36%)
  Pallas kernels  32.1 us (18%)
    ppermute x30, waiting for transfers between devices, swap_block(): return lax.ppermute(v, 'block', [(p, p ^ k) for p in range(n)])  59.6 us
    ppermute x30, starting transfers between devices, swap_block(): return lax.ppermute(v, 'block', [(p, p ^ k) for p in range(n)])  42.9 us
    ppermute x5, waiting for transfers between devices, swap_dp(): return lax.ppermute(v, 'dp', [(p, p ^ bit) for p in range(d)])  19.3 us
    all_to_all x1, starting transfers between devices, per_device(): second = lax.all_to_all(second, 'dp', 0, 0, tiled=True)  10.5 us
    ppermute x5, starting transfers between devices, swap_dp(): return lax.ppermute(v, 'dp', [(p, p ^ bit) for p in range(d)])  9.81 us
    pallas_call x1, Pallas kernels, first_block(): pl.pallas_call(functools.partial(first_kernel, scale, root, n), grid=(nb,...  7.38 us
    pallas_call x1, Pallas kernels, send_h(): pl.pallas_call(functools.partial(send_h_kernel, n), in_specs=[pl.BlockSpe...  6.32 us
    pallas_call x2, Pallas kernels, second_block(): pl.pallas_call(functools.partial(second_kernel, scale, root, n), grid=(co...  5.68 us
  transfers between devices with their start and end apart: 36, of which 14 were waited for; matrix products, arithmetic and copies ran while one was open for 0% of the time, Pallas kernels for 11%

profile of v2, /device:TPU:8, one launch (start us, length us, event | category | flops | bytes accessed | tf_op | source)
XLA Modules:
  0.0 175.2 jit_solution(7768954089765463065)
XLA Ops:
  0.7 5.3 %shard_map.99 = (bf16[8,8,2048]{2,1,0:T(8,128)(2,1)S(1)}, bf16[8,8,2048]{2,1,0:T(8,128)(2,1)S(1)}, bf16[8,8,2048]{2,1,0:T(8,128)(2,1)S(1)}, bf16[8,8,2048]{2,1,0...) custom-call(s32[2]{0:T(128)S(1)} %pad_add_fusion.me_ref, ...), custom_call_target="tpu_custom_call" | custom-call | flops 536870912 | bytes 8388608 | tf_op jit(solution)/shard_map/pallas_call | solution.py:67
  6.1 6.3 %shard_map.100 = (bf16[8,8,8,2048]{3,2,1,0:T(8,128)(2,1)S(1)}, bf16[8,8,8,2048]{3,2,1,0:T(8,128)(2,1)S(1)}) custom-call(s32[2]{0:T(128)S(1)} %pad_add_fusion.me_ref, bf16[8,128,128]{2,1,0:T(8,128)(2,1)S(1)} %copy-done.2, bf16[8,128,2048]{2,1,0:T(8,128)(2,1)} %x_ref.1), custom_call_target="tpu_custom_call" | custom-call | flops 1073741824 | bytes 8388608 | tf_op jit(solution)/shard_map/pallas_call | solution.py:127
  12.5 2.9 %collective-permute-start.1 = (bf16[8,8,2048]{2,1,0:T(8,128)(2,1)S(1)}, bf16[8,8,2048]{2,1,0:T(8,128)(2,1)S(1)}, u32[]{:S(2)}, u32[]{:S(2)}) collective-permute-start(bf16[8,8,2048]{2,1,0:T(8,128)(2,1)S(1)} %get-tuple-element.74), channel_id=1, source_target_pairs={{0,10},{1,11},{2,8},{3,9},{4,14},{5,15},{6,12},{7,13},{8,2},{9,3},... | collective-permute-start | bytes 786440 | tf_op jit(solution)/shard_map/ppermute | solution.py:387
  15.5 2.1 %collective-permute-start.2 = (bf16[8,8,2048]{2,1,0:T(8,128)(2,1)S(1)}, bf16[8,8,2048]{2,1,0:T(8,128)(2,1)S(1)}, u32[]{:S(2)}, u32[]{:S(2)}) collective-permute-start(bf16[8,8,2048]{2,1,0:T(8,128)(2,1)S(1)} %get-tuple-element.75), channel_id=1, source_target_pairs={{0,6},{1,7},{2,4},{3,5},{4,2},{5,3},{6,0},{7,1},{8,14},{9,15},{10,... | collective-permute-start | bytes 786440 | tf_op jit(solution)/shard_map/ppermute | solution.py:387
  18.2 4.5 %collective-permute-done.1.refs_1_ = bf16[8,8,2048]{2,1,0:T(8,128)(2,1)S(1)} collective-permute-done((bf16[8,8,2048]{2,1,0:T(8,128)(2,1)S(1)}, bf16[8,8,2048]{2,1,0:T(8,128)(2,1)S(1)}, u32[]{:S(2)}, u32[]{:S(2)}) %collective-permute-start.1) | collective-permute-done | bytes 262176 | tf_op jit(solution)/shard_map/ppermute | solution.py:387
  24.6 6.0 %collective-permute-done.2.refs_2_ = bf16[8,8,2048]{2,1,0:T(8,128)(2,1)S(1)} collective-permute-done((bf16[8,8,2048]{2,1,0:T(8,128)(2,1)S(1)}, bf16[8,8,2048]{2,1,0:T(8,128)(2,1)S(1)}, u32[]{:S(2)}, u32[]{:S(2)}) %collective-permute-start.2) | collective-permute-done | bytes 262176 | tf_op jit(solution)/shard_map/ppermute | solution.py:387
  33.5 3.4 %collective-permute-start.9 = (bf16[8,8,2048]{2,1,0:T(8,128)(2,1)S(1)}, bf16[8,8,2048]{2,1,0:T(8,128)(2,1)S(1)}, u32[]{:S(2)}, u32[]{:S(2)}) collective-permute-start(bf16[8,8,2048]{2,1,0:T(8,128)(2,1)S(1)} %get-tuple-element.82), channel_id=1, source_target_pairs={{0,7},{1,6},{2,5},{3,4},{4,3},{5,2},{6,1},{7,0},{8,15},{9,14},{10,... | collective-permute-start | bytes 786440 | tf_op jit(solution)/shard_map/ppermute | solution.py:387
  36.9 13.9 %collective-permute-done.6.refs_6_ = bf16[8,8,2048]{2,1,0:T(8,128)(2,1)S(1)} collective-permute-done((bf16[8,8,2048]{2,1,0:T(8,128)(2,1)S(1)}, bf16[8,8,2048]{2,1,0:T(8,128)(2,1)S(1)}, u32[]{:S(2)}, u32[]{:S(2)}) %collective-permute-start.6) | collective-permute-done | bytes 262176 | tf_op jit(solution)/shard_map/ppermute | solution.py:387
  50.8 3.6 %collective-permute-start.12 = (bf16[8,8,2048]{2,1,0:T(8,128)(2,1)S(1)}, bf16[8,8,2048]{2,1,0:T(8,128)(2,1)S(1)}, u32[]{:S(2)}, u32[]{:S(2)}) collective-permute-start(bf16[8,8,2048]{2,1,0:T(8,128)(2,1)S(1)} %get-tuple-element.85), channel_id=1, source_target_pairs={{0,9},{1,8},{2,11},{3,10},{4,13},{5,12},{6,15},{7,14},{8,1},{9,0},... | collective-permute-start | bytes 786440 | tf_op jit(solution)/shard_map/ppermute | solution.py:387
  54.3 2.0 %collective-permute-start.13 = (bf16[8,8,2048]{2,1,0:T(8,128)(2,1)S(1)}, bf16[8,8,2048]{2,1,0:T(8,128)(2,1)S(1)}, u32[]{:S(2)}, u32[]{:S(2)}) collective-permute-start(bf16[8,8,2048]{2,1,0:T(8,128)(2,1)S(1)} %get-tuple-element.86), channel_id=1, source_target_pairs={{0,5},{1,4},{2,7},{3,6},{4,1},{5,0},{6,3},{7,2},{8,13},{9,12},{10,... | collective-permute-start | bytes 786440 | tf_op jit(solution)/shard_map/ppermute | solution.py:387
  56.4 5.3 %collective-permute-done.10.refs_10_ = bf16[8,8,2048]{2,1,0:T(8,128)(2,1)S(1)} collective-permute-done((bf16[8,8,2048]{2,1,0:T(8,128)(2,1)S(1)}, bf16[8,8,2048]{2,1,0:T(8,128)(2,1)S(1)}, u32[]{:S(2)}, u32[]{:S(2)}) %collective-permute-start.10) | collective-permute-done | bytes 262176 | tf_op jit(solution)/shard_map/ppermute | solution.py:387
  62.0 4.9 %collective-permute-start.16 = (bf16[2,4,8,2048]{3,2,1,0:T(8,128)(2,1)S(1)}, bf16[2,4,8,2048]{3,2,1,0:T(8,128)(2,1)S(1)}, u32[]{:S(2)}, u32[]{:S(2)}) collective-permute-start(bf16[2,4,8,2048]{3,2,1,0:T(8,128)(2,1)S(1)} %get-tuple-element.92), channel_id=1, source_target_pairs={{0,10},{1,11},{2,8},{3,9},{4,14},{5,15},{6,12},{7,13},{8,2},{9,3},... | collective-permute-start | bytes 786440 | tf_op jit(solution)/shard_map/ppermute | solution.py:387
  66.9 4.3 %shard_map.102 = (f32[2,4,16,8,128]{4,3,2,1,0:T(8,128)S(1)}, bf16[2,4,16,8,128]{4,3,2,1,0:T(8,128)(2,1)S(1)}) custom-call(s32[2]{0:T(128)S(1)} %pad_add_fusion.me_ref, bf16[8,128,2048]{2,1,0:T(8,128)(2,1)S(1)} %copy-done.1, bf16[8,128,2048]{2,1,0:T(8,128)(2,1)S(1)} %copy-done), custom_call_target="tpu_custom_call" | custom-call | flops 1073741824 | bytes 8388608 | tf_op jit(solution)/shard_map/pallas_call | solution.py:208
  71.7 5.7 %collective-permute-done.13.refs_13_ = bf16[8,8,2048]{2,1,0:T(8,128)(2,1)S(1)} collective-permute-done((bf16[8,8,2048]{2,1,0:T(8,128)(2,1)S(1)}, bf16[8,8,2048]{2,1,0:T(8,128)(2,1)S(1)}, u32[]{:S(2)}, u32[]{:S(2)}) %collective-permute-start.13) | collective-permute-done | bytes 262176 | tf_op jit(solution)/shard_map/ppermute | solution.py:387
  80.6 7.4 %shard_map.103 = (bf16[8,128,2048]{2,1,0:T(8,128)(2,1)}, f32[2,4,32,8,128]{4,3,2,1,0:T(8,128)S(1)}, bf16[2,4,32,8,128]{4,3,2,1,0:T(8,128)(2,1)S(1)}) custom-call(s32[2]{0:T(128)S(1)} %pad_add_fusion.me_ref, bf16[8,128,128]{2,1,0:T(8,128)(2,1)S(1)} %copy-done.2, bf16[8,128,2048]{2,1,0:T(8,128)(2,1)S(1)} %copy-done.1, ...), custom_call_target="tpu_custom_call" | custom-call | flops 2147483648 | bytes 12582912 | tf_op jit(solution)/shard_map/pallas_call | solution.py:251
  87.9 2.3 %collective-permute-start.30 = (bf16[2,4,32,8,128]{4,3,2,1,0:T(8,128)(2,1)S(1)}, bf16[2,4,32,8,128]{4,3,2,1,0:T(8,128)(2,1)S(1)}, u32[]{:S(2)}, u32[]{:S(2)}) collective-permute-start(bf16[2,4,32,8,128]{4,3,2,1,0:T(8,128)(2,1)S(1)} %get-tuple-element.109), channel_id=1, source_target_pairs={{0,128},{16,144},{32,160},{48,176},{64,192},{80,208},{96,224},{112... | collective-permute-start | bytes 1572872 | tf_op jit(solution)/shard_map/ppermute | solution.py:354
  90.2 2.6 %collective-permute-start.21 = (bf16[2,4,8,2048]{3,2,1,0:T(8,128)(2,1)S(1)}, bf16[2,4,8,2048]{3,2,1,0:T(8,128)(2,1)S(1)}, u32[]{:S(2)}, u32[]{:S(2)}) collective-permute-start(bf16[2,4,8,2048]{3,2,1,0:T(8,128)(2,1)S(1)} %get-tuple-element.97), channel_id=1, source_target_pairs={{0,4},{1,5},{2,6},{3,7},{4,0},{5,1},{6,2},{7,3},{8,12},{9,13},{10,... | collective-permute-start | bytes 786440 | tf_op jit(solution)/shard_map/ppermute | solution.py:387
  92.8 2.4 %collective-permute-start.22 = (bf16[2,4,8,2048]{3,2,1,0:T(8,128)(2,1)S(1)}, bf16[2,4,8,2048]{3,2,1,0:T(8,128)(2,1)S(1)}, u32[]{:S(2)}, u32[]{:S(2)}) collective-permute-start(bf16[2,4,8,2048]{3,2,1,0:T(8,128)(2,1)S(1)} %get-tuple-element.98), channel_id=1, source_target_pairs={{0,12},{1,13},{2,14},{3,15},{4,8},{5,9},{6,10},{7,11},{8,4},{9,5},... | collective-permute-start | bytes 786440 | tf_op jit(solution)/shard_map/ppermute | solution.py:387
  95.4 2.5 %collective-permute-start.24 = (bf16[2,4,8,2048]{3,2,1,0:T(8,128)(2,1)S(1)}, bf16[2,4,8,2048]{3,2,1,0:T(8,128)(2,1)S(1)}, u32[]{:S(2)}, u32[]{:S(2)}) collective-permute-start(bf16[2,4,8,2048]{3,2,1,0:T(8,128)(2,1)S(1)} %get-tuple-element.103), channel_id=1, source_target_pairs={{0,6},{1,7},{2,4},{3,5},{4,2},{5,3},{6,0},{7,1},{8,14},{9,15},{10,... | collective-permute-start | bytes 786440 | tf_op jit(solution)/shard_map/ppermute | solution.py:387
  97.8 13.2 %collective-permute-done.21.refs_6_ = bf16[2,4,8,2048]{3,2,1,0:T(8,128)(2,1)S(1)} collective-permute-done((bf16[2,4,8,2048]{3,2,1,0:T(8,128)(2,1)S(1)}, bf16[2,4,8,2048]{3,2,1,0:T(8,128)(2,1)S(1)}, u32[]{:S(2)}, u32[]{:S(2)}) %collective-permute-start.21) | collective-permute-done | bytes 262176 | tf_op jit(solution)/shard_map/ppermute | solution.py:387
  111.1 2.5 %shard_map.104 = (f32[2,4,8,8,128]{4,3,2,1,0:T(8,128)S(1)}, bf16[2,4,8,8,128]{4,3,2,1,0:T(8,128)(2,1)S(1)}) custom-call(s32[2]{0:T(128)S(1)} %pad_add_fusion.me_ref, bf16[8,128,2048]{2,1,0:T(8,128)(2,1)S(1)} %copy-done, bf16[2,4,8,2048]{3,2,1,0:T(8,128)(2,1)S(1)} %get-tuple-element.69.refs_0_, bf16[2,4,8,2048]{3,2,1,0:T(8,128)(2,1)S(1)} %collective-permute-done.16.refs_1_, ...), custom_call_target="tpu_custom_call" | custom-call | flops 536870912 | bytes 4194304 | tf_op jit(solution)/shard_map/pallas_call | solution.py:302
  114.9 2.1 %collective-permute-start.25 = (bf16[2,4,8,2048]{3,2,1,0:T(8,128)(2,1)S(1)}, bf16[2,4,8,2048]{3,2,1,0:T(8,128)(2,1)S(1)}, u32[]{:S(2)}, u32[]{:S(2)}) collective-permute-start(bf16[2,4,8,2048]{3,2,1,0:T(8,128)(2,1)S(1)} %get-tuple-element.104), channel_id=1, source_target_pairs={{0,14},{1,15},{2,12},{3,13},{4,10},{5,11},{6,8},{7,9},{8,6},{9,7},... | collective-permute-start | bytes 786440 | tf_op jit(solution)/shard_map/ppermute | solution.py:387
  118.1 2.0 %collective-permute-done.31.refs_3_ = bf16[2,4,8,8,128]{4,3,2,1,0:T(8,128)(2,1)S(1)} collective-permute-done((bf16[2,4,8,8,128]{4,3,2,1,0:T(8,128)(2,1)S(1)}, bf16[2,4,8,8,128]{4,3,2,1,0:T(8,128)(2,1)S(1)}, u32[]{:S(2)}, u32[]{:S(2)}) %collective-permute-start.31) | collective-permute-done | bytes 131104 | tf_op jit(solution)/shard_map/ppermute | solution.py:354
  120.2 2.5 %collective-permute-start.28 = (bf16[2,4,8,2048]{3,2,1,0:T(8,128)(2,1)S(1)}, bf16[2,4,8,2048]{3,2,1,0:T(8,128)(2,1)S(1)}, u32[]{:S(2)}, u32[]{:S(2)}) collective-permute-start(bf16[2,4,8,2048]{3,2,1,0:T(8,128)(2,1)S(1)} %get-tuple-element.107), channel_id=1, source_target_pairs={{0,4},{1,5},{2,6},{3,7},{4,0},{5,1},{6,2},{7,3},{8,12},{9,13},{10,... | collective-permute-start | bytes 786440 | tf_op jit(solution)/shard_map/ppermute | solution.py:387
  126.9 3.4 %collective-permute-done.27.refs_5_ = bf16[2,4,8,2048]{3,2,1,0:T(8,128)(2,1)S(1)} collective-permute-done((bf16[2,4,8,2048]{3,2,1,0:T(8,128)(2,1)S(1)}, bf16[2,4,8,2048]{3,2,1,0:T(8,128)(2,1)S(1)}, u32[]{:S(2)}, u32[]{:S(2)}) %collective-permute-start.27) | collective-permute-done | bytes 262176 | tf_op jit(solution)/shard_map/ppermute | solution.py:387
  130.3 3.0 %collective-permute-done.28.refs_6_ = bf16[2,4,8,2048]{3,2,1,0:T(8,128)(2,1)S(1)} collective-permute-done((bf16[2,4,8,2048]{3,2,1,0:T(8,128)(2,1)S(1)}, bf16[2,4,8,2048]{3,2,1,0:T(8,128)(2,1)S(1)}, u32[]{:S(2)}, u32[]{:S(2)}) %collective-permute-start.28) | collective-permute-done | bytes 262176 | tf_op jit(solution)/shard_map/ppermute | solution.py:387
  133.3 3.4 %collective-permute-done.29.refs_7_ = bf16[2,4,8,2048]{3,2,1,0:T(8,128)(2,1)S(1)} collective-permute-done((bf16[2,4,8,2048]{3,2,1,0:T(8,128)(2,1)S(1)}, bf16[2,4,8,2048]{3,2,1,0:T(8,128)(2,1)S(1)}, u32[]{:S(2)}, u32[]{:S(2)}) %collective-permute-start.29) | collective-permute-done | bytes 262176 | tf_op jit(solution)/shard_map/ppermute | solution.py:387
  136.7 3.1 %shard_map.105 = bf16[16,2,4,8,128]{4,3,2,1,0:T(8,128)(2,1)} custom-call(s32[2]{0:T(128)S(1)} %pad_add_fusion.me_ref, bf16[8,128,2048]{2,1,0:T(8,128)(2,1)S(1)} %copy-done, bf16[2,4,8,2048]{3,2,1,0:T(8,128)(2,1)S(1)} %get-tuple-element.101.refs_0_, bf16[2,4,8,2048]{3,2,1,0:T(8,128)(2,1)S(1)} %collective-permute-done.23.refs_1_, ...), custom_call_target="tpu_custom_call" | custom-call | flops 536870912 | bytes 4194304 | tf_op jit(solution)/shard_map/pallas_call | solution.py:302
  139.8 10.5 %all-to-all-start = ((bf16[16,2,4,8,128]{4,3,2,1,0:T(8,128)(2,1)}), bf16[16,2,4,8,128]{4,3,2,1,0:T(8,128)(2,1)S(1)}, u32[]{:S(2)}, u32[]{:S(2)}) async-start(bf16[16,2,4,8,128]{4,3,2,1,0:T(8,128)(2,1)} %shard_map.105), calls=%async_computation | async-start | bytes 524288 | tf_op jit(solution)/shard_map/all_to_all | solution.py:437
  151.0 5.5 %collective-permute-start.33 = (bf16[2,40,8,128]{3,2,1,0:T(8,128)(2,1)S(1)}, bf16[2,40,8,128]{3,2,1,0:T(8,128)(2,1)S(1)}, u32[]{:S(2)}, u32[]{:S(2)}) collective-permute-start(bf16[2,40,8,128]{3,2,1,0:T(8,128)(2,1)S(1)} %get-tuple-element.114), channel_id=1, source_target_pairs={{0,32},{16,48},{32,0},{48,16},{64,96},{80,112},{96,64},{112,80},{1... | collective-permute-start | bytes 491528 | tf_op jit(solution)/shard_map/ppermute | solution.py:354
  156.5 11.1 %collective-permute-done.33.refs_1_ = bf16[2,40,8,128]{3,2,1,0:T(8,128)(2,1)S(1)} collective-permute-done((bf16[2,40,8,128]{3,2,1,0:T(8,128)(2,1)S(1)}, bf16[2,40,8,128]{3,2,1,0:T(8,128)(2,1)S(1)}, u32[]{:S(2)}, u32[]{:S(2)}) %collective-permute-start.33) | collective-permute-done | bytes 163872 | tf_op jit(solution)/shard_map/ppermute | solution.py:354
  168.3 6.2 %collective-permute-done.34.got_ref = bf16[40,8,128]{2,1,0:T(8,128)(2,1)S(1)} collective-permute-done((bf16[40,8,128]{2,1,0:T(8,128)(2,1)S(1)}, bf16[40,8,128]{2,1,0:T(8,128)(2,1)S(1)}, u32[]{:S(2)}, u32[]{:S(2)}) %collective-permute-start.34) | collective-permute-done | bytes 81952 | tf_op jit(solution)/shard_map/ppermute | solution.py:354
  (58 shorter events, 18.4 us)
Async XLA Ops:
  12.4 49.2 %collective-permute-start = (bf16[8,8,8,2048]{3,2,1,0:T(8,128)(2,1)S(1)}, bf16[8,8,8,2048]{3,2,1,0:T(8,128)(2,1)S(1)}, u32[]{:S(2)}, u32[]{:S(2)}) collective-permute-start(bf16[8,8,8,2048]{3,2,1,0:T(8,128)(2,1)S(1)} %get-tuple-element.68), channel_id=1, source_target_pairs={{0,1},{1,0},{2,3},{3,2},{4,5},{5,4},{6,7},{7,6},{8,9},{9,8},{10,11... | collective-permute-start | bytes 6291464 | tf_op jit(solution)/shard_map/ppermute | solution.py:387
  15.5 15.2 %collective-permute-start.2 = (bf16[8,8,2048]{2,1,0:T(8,128)(2,1)S(1)}, bf16[8,8,2048]{2,1,0:T(8,128)(2,1)S(1)}, u32[]{:S(2)}, u32[]{:S(2)}) collective-permute-start(bf16[8,8,2048]{2,1,0:T(8,128)(2,1)S(1)} %get-tuple-element.75), channel_id=1, source_target_pairs={{0,6},{1,7},{2,4},{3,5},{4,2},{5,3},{6,0},{7,1},{8,14},{9,15},{10,... | collective-permute-start | bytes 786440 | tf_op jit(solution)/shard_map/ppermute | solution.py:387
  17.6 14.6 %collective-permute-start.3 = (bf16[8,8,2048]{2,1,0:T(8,128)(2,1)S(1)}, bf16[8,8,2048]{2,1,0:T(8,128)(2,1)S(1)}, u32[]{:S(2)}, u32[]{:S(2)}) collective-permute-start(bf16[8,8,2048]{2,1,0:T(8,128)(2,1)S(1)} %get-tuple-element.76), channel_id=1, source_target_pairs={{0,14},{1,15},{2,12},{3,13},{4,10},{5,11},{6,8},{7,9},{8,6},{9,7},... | collective-permute-start | bytes 786440 | tf_op jit(solution)/shard_map/ppermute | solution.py:387
  18.2 14.0 %collective-permute-start.4 = (bf16[8,8,2048]{2,1,0:T(8,128)(2,1)S(1)}, bf16[8,8,2048]{2,1,0:T(8,128)(2,1)S(1)}, u32[]{:S(2)}, u32[]{:S(2)}) collective-permute-start(bf16[8,8,2048]{2,1,0:T(8,128)(2,1)S(1)} %get-tuple-element.77), channel_id=1, source_target_pairs={{0,2},{1,3},{2,0},{3,1},{4,6},{5,7},{6,4},{7,5},{8,10},{9,11},{10,... | collective-permute-start | bytes 786440 | tf_op jit(solution)/shard_map/ppermute | solution.py:387
  22.7 10.8 %collective-permute-start.5 = (bf16[8,8,2048]{2,1,0:T(8,128)(2,1)S(1)}, bf16[8,8,2048]{2,1,0:T(8,128)(2,1)S(1)}, u32[]{:S(2)}, u32[]{:S(2)}) collective-permute-start(bf16[8,8,2048]{2,1,0:T(8,128)(2,1)S(1)} %get-tuple-element.78), channel_id=1, source_target_pairs={{0,8},{1,9},{2,10},{3,11},{4,12},{5,13},{6,14},{7,15},{8,0},{9,1},... | collective-permute-start | bytes 786440 | tf_op jit(solution)/shard_map/ppermute | solution.py:387
  30.6 20.1 %collective-permute-start.6 = (bf16[8,8,2048]{2,1,0:T(8,128)(2,1)S(1)}, bf16[8,8,2048]{2,1,0:T(8,128)(2,1)S(1)}, u32[]{:S(2)}, u32[]{:S(2)}) collective-permute-start(bf16[8,8,2048]{2,1,0:T(8,128)(2,1)S(1)} %get-tuple-element.79), channel_id=1, source_target_pairs={{0,4},{1,5},{2,6},{3,7},{4,0},{5,1},{6,2},{7,3},{8,12},{9,13},{10,... | collective-permute-start | bytes 786440 | tf_op jit(solution)/shard_map/ppermute | solution.py:387
  32.1 18.6 %collective-permute-start.7 = (bf16[8,8,2048]{2,1,0:T(8,128)(2,1)S(1)}, bf16[8,8,2048]{2,1,0:T(8,128)(2,1)S(1)}, u32[]{:S(2)}, u32[]{:S(2)}) collective-permute-start(bf16[8,8,2048]{2,1,0:T(8,128)(2,1)S(1)} %get-tuple-element.80), channel_id=1, source_target_pairs={{0,12},{1,13},{2,14},{3,15},{4,8},{5,9},{6,10},{7,11},{8,4},{9,5},... | collective-permute-start | bytes 786440 | tf_op jit(solution)/shard_map/ppermute | solution.py:387
  32.2 18.6 %collective-permute-start.8 = (bf16[8,8,2048]{2,1,0:T(8,128)(2,1)S(1)}, bf16[8,8,2048]{2,1,0:T(8,128)(2,1)S(1)}, u32[]{:S(2)}, u32[]{:S(2)}) collective-permute-start(bf16[8,8,2048]{2,1,0:T(8,128)(2,1)S(1)} %get-tuple-element.81), channel_id=1, source_target_pairs={{0,11},{1,10},{2,9},{3,8},{4,15},{5,14},{6,13},{7,12},{8,3},{9,2},... | collective-permute-start | bytes 786440 | tf_op jit(solution)/shard_map/ppermute | solution.py:387
  33.5 20.9 %collective-permute-start.9 = (bf16[8,8,2048]{2,1,0:T(8,128)(2,1)S(1)}, bf16[8,8,2048]{2,1,0:T(8,128)(2,1)S(1)}, u32[]{:S(2)}, u32[]{:S(2)}) collective-permute-start(bf16[8,8,2048]{2,1,0:T(8,128)(2,1)S(1)} %get-tuple-element.82), channel_id=1, source_target_pairs={{0,7},{1,6},{2,5},{3,4},{4,3},{5,2},{6,1},{7,0},{8,15},{9,14},{10,... | collective-permute-start | bytes 786440 | tf_op jit(solution)/shard_map/ppermute | solution.py:387
  50.7 10.9 %collective-permute-start.10 = (bf16[8,8,2048]{2,1,0:T(8,128)(2,1)S(1)}, bf16[8,8,2048]{2,1,0:T(8,128)(2,1)S(1)}, u32[]{:S(2)}, u32[]{:S(2)}) collective-permute-start(bf16[8,8,2048]{2,1,0:T(8,128)(2,1)S(1)} %get-tuple-element.83), channel_id=1, source_target_pairs={{0,15},{1,14},{2,13},{3,12},{4,11},{5,10},{6,9},{7,8},{8,7},{9,6},... | collective-permute-start | bytes 786440 | tf_op jit(solution)/shard_map/ppermute | solution.py:387
  50.8 11.2 %collective-permute-start.11 = (bf16[8,8,2048]{2,1,0:T(8,128)(2,1)S(1)}, bf16[8,8,2048]{2,1,0:T(8,128)(2,1)S(1)}, u32[]{:S(2)}, u32[]{:S(2)}) collective-permute-start(bf16[8,8,2048]{2,1,0:T(8,128)(2,1)S(1)} %get-tuple-element.84), channel_id=1, source_target_pairs={{0,3},{1,2},{2,1},{3,0},{4,7},{5,6},{6,5},{7,4},{8,11},{9,10},{10,... | collective-permute-start | bytes 786440 | tf_op jit(solution)/shard_map/ppermute | solution.py:387
  50.8 20.4 %collective-permute-start.12 = (bf16[8,8,2048]{2,1,0:T(8,128)(2,1)S(1)}, bf16[8,8,2048]{2,1,0:T(8,128)(2,1)S(1)}, u32[]{:S(2)}, u32[]{:S(2)}) collective-permute-start(bf16[8,8,2048]{2,1,0:T(8,128)(2,1)S(1)} %get-tuple-element.85), channel_id=1, source_target_pairs={{0,9},{1,8},{2,11},{3,10},{4,13},{5,12},{6,15},{7,14},{8,1},{9,0},... | collective-permute-start | bytes 786440 | tf_op jit(solution)/shard_map/ppermute | solution.py:387
  54.3 23.1 %collective-permute-start.13 = (bf16[8,8,2048]{2,1,0:T(8,128)(2,1)S(1)}, bf16[8,8,2048]{2,1,0:T(8,128)(2,1)S(1)}, u32[]{:S(2)}, u32[]{:S(2)}) collective-permute-start(bf16[8,8,2048]{2,1,0:T(8,128)(2,1)S(1)} %get-tuple-element.86), channel_id=1, source_target_pairs={{0,5},{1,4},{2,7},{3,6},{4,1},{5,0},{6,3},{7,2},{8,13},{9,12},{10,... | collective-permute-start | bytes 786440 | tf_op jit(solution)/shard_map/ppermute | solution.py:387
  61.6 17.6 %collective-permute-start.14 = (bf16[8,8,2048]{2,1,0:T(8,128)(2,1)S(1)}, bf16[8,8,2048]{2,1,0:T(8,128)(2,1)S(1)}, u32[]{:S(2)}, u32[]{:S(2)}) collective-permute-start(bf16[8,8,2048]{2,1,0:T(8,128)(2,1)S(1)} %get-tuple-element.87), channel_id=1, source_target_pairs={{0,13},{1,12},{2,15},{3,14},{4,9},{5,8},{6,11},{7,10},{8,5},{9,4},... | collective-permute-start | bytes 786440 | tf_op jit(solution)/shard_map/ppermute | solution.py:387
  61.6 18.9 %collective-permute-start.15 = (bf16[8,8,2048]{2,1,0:T(8,128)(2,1)S(1)}, bf16[8,8,2048]{2,1,0:T(8,128)(2,1)S(1)}, u32[]{:S(2)}, u32[]{:S(2)}) collective-permute-start(bf16[8,8,2048]{2,1,0:T(8,128)(2,1)S(1)} %get-tuple-element.88), channel_id=1, source_target_pairs={{0,1},{1,0},{2,3},{3,2},{4,5},{5,4},{6,7},{7,6},{8,9},{9,8},{10,11... | collective-permute-start | bytes 786440 | tf_op jit(solution)/shard_map/ppermute | solution.py:387
  62.0 26.0 %collective-permute-start.16 = (bf16[2,4,8,2048]{3,2,1,0:T(8,128)(2,1)S(1)}, bf16[2,4,8,2048]{3,2,1,0:T(8,128)(2,1)S(1)}, u32[]{:S(2)}, u32[]{:S(2)}) collective-permute-start(bf16[2,4,8,2048]{3,2,1,0:T(8,128)(2,1)S(1)} %get-tuple-element.92), channel_id=1, source_target_pairs={{0,10},{1,11},{2,8},{3,9},{4,14},{5,15},{6,12},{7,13},{8,2},{9,3},... | collective-permute-start | bytes 786440 | tf_op jit(solution)/shard_map/ppermute | solution.py:387
  71.2 19.0 %collective-permute-start.17 = (bf16[2,4,8,2048]{3,2,1,0:T(8,128)(2,1)S(1)}, bf16[2,4,8,2048]{3,2,1,0:T(8,128)(2,1)S(1)}, u32[]{:S(2)}, u32[]{:S(2)}) collective-permute-start(bf16[2,4,8,2048]{3,2,1,0:T(8,128)(2,1)S(1)} %get-tuple-element.93), channel_id=1, source_target_pairs={{0,6},{1,7},{2,4},{3,5},{4,2},{5,3},{6,0},{7,1},{8,14},{9,15},{10,... | collective-permute-start | bytes 786440 | tf_op jit(solution)/shard_map/ppermute | solution.py:387
  77.4 15.4 %collective-permute-start.18 = (bf16[2,4,8,2048]{3,2,1,0:T(8,128)(2,1)S(1)}, bf16[2,4,8,2048]{3,2,1,0:T(8,128)(2,1)S(1)}, u32[]{:S(2)}, u32[]{:S(2)}) collective-permute-start(bf16[2,4,8,2048]{3,2,1,0:T(8,128)(2,1)S(1)} %get-tuple-element.94), channel_id=1, source_target_pairs={{0,14},{1,15},{2,12},{3,13},{4,10},{5,11},{6,8},{7,9},{8,6},{9,7},... | collective-permute-start | bytes 786440 | tf_op jit(solution)/shard_map/ppermute | solution.py:387
  79.2 16.0 %collective-permute-start.19 = (bf16[2,4,8,2048]{3,2,1,0:T(8,128)(2,1)S(1)}, bf16[2,4,8,2048]{3,2,1,0:T(8,128)(2,1)S(1)}, u32[]{:S(2)}, u32[]{:S(2)}) collective-permute-start(bf16[2,4,8,2048]{3,2,1,0:T(8,128)(2,1)S(1)} %get-tuple-element.95), channel_id=1, source_target_pairs={{0,2},{1,3},{2,0},{3,1},{4,6},{5,7},{6,4},{7,5},{8,10},{9,11},{10,... | collective-permute-start | bytes 786440 | tf_op jit(solution)/shard_map/ppermute | solution.py:387
  80.6 14.8 %collective-permute-start.20 = (bf16[2,4,8,2048]{3,2,1,0:T(8,128)(2,1)S(1)}, bf16[2,4,8,2048]{3,2,1,0:T(8,128)(2,1)S(1)}, u32[]{:S(2)}, u32[]{:S(2)}) collective-permute-start(bf16[2,4,8,2048]{3,2,1,0:T(8,128)(2,1)S(1)} %get-tuple-element.96), channel_id=1, source_target_pairs={{0,8},{1,9},{2,10},{3,11},{4,12},{5,13},{6,14},{7,15},{8,0},{9,1},... | collective-permute-start | bytes 786440 | tf_op jit(solution)/shard_map/ppermute | solution.py:387
  87.9 34.7 %collective-permute-start.30 = (bf16[2,4,32,8,128]{4,3,2,1,0:T(8,128)(2,1)S(1)}, bf16[2,4,32,8,128]{4,3,2,1,0:T(8,128)(2,1)S(1)}, u32[]{:S(2)}, u32[]{:S(2)}) collective-permute-start(bf16[2,4,32,8,128]{4,3,2,1,0:T(8,128)(2,1)S(1)} %get-tuple-element.109), channel_id=1, source_target_pairs={{0,128},{16,144},{32,160},{48,176},{64,192},{80,208},{96,224},{112... | collective-permute-start | bytes 1572872 | tf_op jit(solution)/shard_map/ppermute | solution.py:354
  90.2 20.8 %collective-permute-start.21 = (bf16[2,4,8,2048]{3,2,1,0:T(8,128)(2,1)S(1)}, bf16[2,4,8,2048]{3,2,1,0:T(8,128)(2,1)S(1)}, u32[]{:S(2)}, u32[]{:S(2)}) collective-permute-start(bf16[2,4,8,2048]{3,2,1,0:T(8,128)(2,1)S(1)} %get-tuple-element.97), channel_id=1, source_target_pairs={{0,4},{1,5},{2,6},{3,7},{4,0},{5,1},{6,2},{7,3},{8,12},{9,13},{10,... | collective-permute-start | bytes 786440 | tf_op jit(solution)/shard_map/ppermute | solution.py:387
  92.8 18.2 %collective-permute-start.22 = (bf16[2,4,8,2048]{3,2,1,0:T(8,128)(2,1)S(1)}, bf16[2,4,8,2048]{3,2,1,0:T(8,128)(2,1)S(1)}, u32[]{:S(2)}, u32[]{:S(2)}) collective-permute-start(bf16[2,4,8,2048]{3,2,1,0:T(8,128)(2,1)S(1)} %get-tuple-element.98), channel_id=1, source_target_pairs={{0,12},{1,13},{2,14},{3,15},{4,8},{5,9},{6,10},{7,11},{8,4},{9,5},... | collective-permute-start | bytes 786440 | tf_op jit(solution)/shard_map/ppermute | solution.py:387
  95.2 21.8 %collective-permute-start.23 = (bf16[2,4,8,2048]{3,2,1,0:T(8,128)(2,1)S(1)}, bf16[2,4,8,2048]{3,2,1,0:T(8,128)(2,1)S(1)}, u32[]{:S(2)}, u32[]{:S(2)}) collective-permute-start(bf16[2,4,8,2048]{3,2,1,0:T(8,128)(2,1)S(1)} %get-tuple-element.102), channel_id=1, source_target_pairs={{0,10},{1,11},{2,8},{3,9},{4,14},{5,15},{6,12},{7,13},{8,2},{9,3},... | collective-permute-start | bytes 786440 | tf_op jit(solution)/shard_map/ppermute | solution.py:387
  95.4 21.8 %collective-permute-start.24 = (bf16[2,4,8,2048]{3,2,1,0:T(8,128)(2,1)S(1)}, bf16[2,4,8,2048]{3,2,1,0:T(8,128)(2,1)S(1)}, u32[]{:S(2)}, u32[]{:S(2)}) collective-permute-start(bf16[2,4,8,2048]{3,2,1,0:T(8,128)(2,1)S(1)} %get-tuple-element.103), channel_id=1, source_target_pairs={{0,6},{1,7},{2,4},{3,5},{4,2},{5,3},{6,0},{7,1},{8,14},{9,15},{10,... | collective-permute-start | bytes 786440 | tf_op jit(solution)/shard_map/ppermute | solution.py:387
  114.9 11.3 %collective-permute-start.25 = (bf16[2,4,8,2048]{3,2,1,0:T(8,128)(2,1)S(1)}, bf16[2,4,8,2048]{3,2,1,0:T(8,128)(2,1)S(1)}, u32[]{:S(2)}, u32[]{:S(2)}) collective-permute-start(bf16[2,4,8,2048]{3,2,1,0:T(8,128)(2,1)S(1)} %get-tuple-element.104), channel_id=1, source_target_pairs={{0,14},{1,15},{2,12},{3,13},{4,10},{5,11},{6,8},{7,9},{8,6},{9,7},... | collective-permute-start | bytes 786440 | tf_op jit(solution)/shard_map/ppermute | solution.py:387
  117.1 13.1 %collective-permute-start.27 = (bf16[2,4,8,2048]{3,2,1,0:T(8,128)(2,1)S(1)}, bf16[2,4,8,2048]{3,2,1,0:T(8,128)(2,1)S(1)}, u32[]{:S(2)}, u32[]{:S(2)}) collective-permute-start(bf16[2,4,8,2048]{3,2,1,0:T(8,128)(2,1)S(1)} %get-tuple-element.106), channel_id=1, source_target_pairs={{0,8},{1,9},{2,10},{3,11},{4,12},{5,13},{6,14},{7,15},{8,0},{9,1},... | collective-permute-start | bytes 786440 | tf_op jit(solution)/shard_map/ppermute | solution.py:387
  120.2 13.1 %collective-permute-start.28 = (bf16[2,4,8,2048]{3,2,1,0:T(8,128)(2,1)S(1)}, bf16[2,4,8,2048]{3,2,1,0:T(8,128)(2,1)S(1)}, u32[]{:S(2)}, u32[]{:S(2)}) collective-permute-start(bf16[2,4,8,2048]{3,2,1,0:T(8,128)(2,1)S(1)} %get-tuple-element.107), channel_id=1, source_target_pairs={{0,4},{1,5},{2,6},{3,7},{4,0},{5,1},{6,2},{7,3},{8,12},{9,13},{10,... | collective-permute-start | bytes 786440 | tf_op jit(solution)/shard_map/ppermute | solution.py:387
  122.7 14.0 %collective-permute-start.29 = (bf16[2,4,8,2048]{3,2,1,0:T(8,128)(2,1)S(1)}, bf16[2,4,8,2048]{3,2,1,0:T(8,128)(2,1)S(1)}, u32[]{:S(2)}, u32[]{:S(2)}) collective-permute-start(bf16[2,4,8,2048]{3,2,1,0:T(8,128)(2,1)S(1)} %get-tuple-element.108), channel_id=1, source_target_pairs={{0,12},{1,13},{2,14},{3,15},{4,8},{5,9},{6,10},{7,11},{8,4},{9,5},... | collective-permute-start | bytes 786440 | tf_op jit(solution)/shard_map/ppermute | solution.py:387
  126.2 24.1 %collective-permute-start.32 = (bf16[4,40,8,128]{3,2,1,0:T(8,128)(2,1)S(1)}, bf16[4,40,8,128]{3,2,1,0:T(8,128)(2,1)S(1)}, u32[]{:S(2)}, u32[]{:S(2)}) collective-permute-start(bf16[4,40,8,128]{3,2,1,0:T(8,128)(2,1)S(1)} %get-tuple-element.112), channel_id=1, source_target_pairs={{0,64},{16,80},{32,96},{48,112},{64,0},{80,16},{96,32},{112,48},{1... | collective-permute-start | bytes 983048 | tf_op jit(solution)/shard_map/ppermute | solution.py:354
  139.8 28.5 %all-to-all-start = ((bf16[16,2,4,8,128]{4,3,2,1,0:T(8,128)(2,1)}), bf16[16,2,4,8,128]{4,3,2,1,0:T(8,128)(2,1)S(1)}, u32[]{:S(2)}, u32[]{:S(2)}) async-start(bf16[16,2,4,8,128]{4,3,2,1,0:T(8,128)(2,1)} %shard_map.105), calls=%async_computation | async-start | bytes 524288 | tf_op jit(solution)/shard_map/all_to_all | solution.py:437
  151.0 16.6 %collective-permute-start.33 = (bf16[2,40,8,128]{3,2,1,0:T(8,128)(2,1)S(1)}, bf16[2,40,8,128]{3,2,1,0:T(8,128)(2,1)S(1)}, u32[]{:S(2)}, u32[]{:S(2)}) collective-permute-start(bf16[2,40,8,128]{3,2,1,0:T(8,128)(2,1)S(1)} %get-tuple-element.114), channel_id=1, source_target_pairs={{0,32},{16,48},{32,0},{48,16},{64,96},{80,112},{96,64},{112,80},{1... | collective-permute-start | bytes 491528 | tf_op jit(solution)/shard_map/ppermute | solution.py:354
  (7 other events, 160.0 us)

commit v3 on v2

--- a/solution.py
+++ b/solution.py
@@ -32,16 +32,16 @@
     return pltpu.make_async_copy(src.at[b], dst.at[b], sems.at[b])
 
 
-def mix(weights_at, n, me, wbuf):
-    for k in range(n):
-        wbuf[k] = weights_at(me ^ k)
+def mix(weights_at, steps, me, wbuf):
+    for m, k in enumerate(steps):
+        wbuf[m] = weights_at(me ^ k)
     a, b, c = wbuf.shape
     return wbuf[...].reshape(a * b, c)
 
 
-def send_g_kernel(me_ref, w_ref, c_hbm, *refs):
-    n = w_ref.shape[1]
-    outs, (cbuf, wall, wbuf, sems, wsem) = refs[:n], refs[n:]
+def send_g_kernel(steps, me_ref, w_ref, c_hbm, *refs):
+    count = len(steps)
+    outs, (cbuf, wall, wbuf, sems, wsem) = refs[:count], refs[count:]
     nb, _, rows, _ = w_ref.shape
     me = me_ref[0]
     weights = pltpu.make_async_copy(w_ref, wall, wsem)
@@ -51,37 +51,38 @@
     weights.wait()
 
     def step(j, carry):
-        w = mix(lambda d: wall[j, d], n, me, wbuf)
+        w = mix(lambda d: wall[j, d], steps, me, wbuf)
         fetch(c_hbm, cbuf, sems, j).wait()
         r = jnp.dot(w, cbuf[j], preferred_element_type=F32)
-        for k in range(n):
-            outs[k][j] = r[k * rows : (k + 1) * rows].astype(BF)
+        for m in range(count):
+            outs[m][j] = r[m * rows : (m + 1) * rows].astype(BF)
         return carry
 
     lax.fori_loop(0, nb, step, 0)
 
 
-def send_g(me, w_second, cotangent, n):
+def send_g(me, w_second, cotangent, n, steps):
     nb, bs, t = cotangent.shape
     rows = bs // n
-    return pl.pallas_call(
-        send_g_kernel,
+    count = len(steps)
+    return pl.pallas_call(
+        functools.partial(send_g_kernel, steps),
         in_specs=[
             pl.BlockSpec(memory_space=SMEM),
             pl.BlockSpec(memory_space=pltpu.HBM),
             pl.BlockSpec(memory_space=pltpu.HBM),
         ],
-        out_specs=[pl.BlockSpec(memory_space=VMEM)] * n,
-        out_shape=[pltpu.VMEM((nb, rows, t), BF)] * n,
+        out_specs=[pl.BlockSpec(memory_space=VMEM)] * count,
+        out_shape=[pltpu.VMEM((nb, rows, t), BF)] * count,
         scratch_shapes=[
             pltpu.VMEM((nb, bs, t), BF),
             pltpu.VMEM((nb, n, rows, bs), BF),
-            pltpu.VMEM((n, rows, bs), BF),
+            pltpu.VMEM((count, rows, bs), BF),
             pltpu.SemaphoreType.DMA((nb,)),
             pltpu.SemaphoreType.DMA,
         ],
         compiler_params=params(12),
-        cost_estimate=cost(2 * nb * bs * bs * t, 4 * nb * bs * t),
+        cost_estimate=cost(2 * nb * count * rows * bs * t, 4 * nb * bs * t),
     )(me, in_hbm(w_second.reshape(nb, n, rows, bs)), in_hbm(cotangent))
 
 
@@ -105,7 +106,7 @@
 
     def step(i, carry):
         wt[...] = w_ref[i].astype(F32).T.reshape(n, rows, bs).astype(BF)
-        w = mix(lambda d: wt[d], n, me, wbuf)
+        w = mix(lambda d: wt[d], range(n), me, wbuf)
         fetch(x_hbm, xbuf, sems, i).wait()
         r = jnp.dot(w, xbuf[i], preferred_element_type=F32)
         for k in range(n):
@@ -169,8 +170,9 @@
 
 
 NY = 4
-ORDER = (10, 6, 14, 2, 8, 4, 12, 11, 7, 15, 3, 9, 5, 13, 1)
+ORDER = (12, 10, 6, 14, 2, 8, 4, 1, 11, 7, 15, 3, 9, 5, 13)
 ISSUE = (0,) + ORDER
+SOON, LATER = ORDER[:7], ORDER[7:] + (0,)
 CHIPS = (0, 5, 3, 7, 1, 4, 2, 6)
 PARTS = 2
 
@@ -387,9 +389,9 @@
     return lax.ppermute(v, "block", [(p, p ^ k) for p in range(n)])
 
 
-def exchange(pieces):
-    got = [pieces[0]] + [swap_block(pieces[k], k) for k in range(1, len(pieces))]
-    return [pltpu.with_memory_space_constraint(v, pltpu.VMEM) for v in got]
+def exchange(steps, pieces):
+    got = {k: v if k == 0 else swap_block(v, k) for k, v in zip(steps, pieces)}
+    return {k: pltpu.with_memory_space_constraint(v, pltpu.VMEM) for k, v in got.items()}
 
 
 def exchange_chips(pieces):
@@ -412,9 +414,12 @@
     def after(v, *done):
         return lax.optimization_barrier((v,) + done)[0]
 
-    out_g = send_g(me, w_second, cotangent, n)
-    got_g = exchange(out_g)
-    own, other = send_h(me, w_first, after(layer_input, out_g[0]), n)
+    out_g1 = send_g(me, w_second, cotangent, n, SOON)
+    got_g1 = exchange(SOON, out_g1)
+    out_g2 = send_g(me, w_second, after(cotangent, out_g1[0]), n, LATER)
+    got_g2 = exchange(LATER, out_g2)
+    got_g = [(got_g1 | got_g2)[k] for k in range(n)]
+    own, other = send_h(me, w_first, after(layer_input, out_g2[0]), n)
     other = swap_block(other, 1)
     local = local_stats(me, after(layer_input, own), cotangent, scale, d)
     packed = pack(own, pltpu.with_memory_space_constraint(other, pltpu.VMEM))

time: 175 us -> 179 us (1.023)
  the two profiles are of different devices: /device:TPU:8 before, /device:TPU:2 now
where the time goes in v3:
time: 179 us; the launch traced here: 177 us
  waiting for transfers between devices  75.2 us (42%)
  starting transfers between devices  65 us (36%)
  Pallas kernels  36 us (20%)
    ppermute x30, waiting for transfers between devices, swap_block(): return lax.ppermute(v, 'block', [(p, p ^ k) for p in range(n)])  56.2 us
    ppermute x30, starting transfers between devices, swap_block(): return lax.ppermute(v, 'block', [(p, p ^ k) for p in range(n)])  43.9 us
    ppermute x5, waiting for transfers between devices, swap_dp(): return lax.ppermute(v, 'dp', [(p, p ^ bit) for p in range(d)])  19 us
    ppermute x5, starting transfers between devices, swap_dp(): return lax.ppermute(v, 'dp', [(p, p ^ bit) for p in range(d)])  11.1 us
    all_to_all x1, starting transfers between devices, per_device(): second = lax.all_to_all(second, 'dp', 0, 0, tiled=True)  9.96 us
    pallas_call x2, Pallas kernels, send_g(): pl.pallas_call(functools.partial(send_g_kernel, steps), in_specs=[pl.Bloc...  9.3 us
    pallas_call x1, Pallas kernels, first_block(): pl.pallas_call(functools.partial(first_kernel, scale, root, n), grid=(nb,...  7.4 us
    pallas_call x1, Pallas kernels, send_h(): pl.pallas_call(functools.partial(send_h_kernel, n), in_specs=[pl.BlockSpe...  6.29 us
  transfers between devices with their start and end apart: 36, of which 12 were waited for; matrix products, arithmetic and copies ran while one was open for 0% of the time, Pallas kernels for 11%

profile of v3, /device:TPU:2, one launch (start us, length us, event | category | flops | bytes accessed | tf_op | source)
XLA Modules:
  0.0 177.1 jit_solution(11500916455758747346)
XLA Ops:
  0.7 4.6 %shard_map.99 = (bf16[8,8,2048]{2,1,0:T(8,128)(2,1)S(1)}, bf16[8,8,2048]{2,1,0:T(8,128)(2,1)S(1)}, bf16[8,8,2048]{2,1,0:T(8,128)(2,1)S(1)}, bf16[8,8,2048]{2,1,0...) custom-call(s32[2]{0:T(128)S(1)} %pad_add_fusion.me_ref, ...), custom_call_target="tpu_custom_call" | custom-call | flops 234881024 | bytes 8388608 | tf_op jit(solution)/shard_map/pallas_call | solution.py:68
  5.3 4.7 %shard_map.100 = (bf16[8,8,2048]{2,1,0:T(8,128)(2,1)S(1)}, bf16[8,8,2048]{2,1,0:T(8,128)(2,1)S(1)}, bf16[8,8,2048]{2,1,0:T(8,128)(2,1)S(1)}, bf16[8,8,2048]{2,1,...) custom-call(s32[2]{0:T(128)S(1)} %pad_add_fusion.me_ref, ...), custom_call_target="tpu_custom_call" | custom-call | flops 301989888 | bytes 8388608 | tf_op jit(solution)/shard_map/pallas_call | solution.py:68
  10.1 6.3 %shard_map.101 = (bf16[8,8,8,2048]{3,2,1,0:T(8,128)(2,1)S(1)}, bf16[8,8,8,2048]{3,2,1,0:T(8,128)(2,1)S(1)}) custom-call(s32[2]{0:T(128)S(1)} %pad_add_fusion.me_ref, bf16[8,128,128]{2,1,0:T(8,128)(2,1)S(1)} %copy-done.2, bf16[8,128,2048]{2,1,0:T(8,128)(2,1)} %x_ref.1), custom_call_target="tpu_custom_call" | custom-call | flops 1073741824 | bytes 8388608 | tf_op jit(solution)/shard_map/pallas_call | solution.py:128
  16.5 2.0 %collective-permute-start.2 = (bf16[8,8,2048]{2,1,0:T(8,128)(2,1)S(1)}, bf16[8,8,2048]{2,1,0:T(8,128)(2,1)S(1)}, u32[]{:S(2)}, u32[]{:S(2)}) collective-permute-start(bf16[8,8,2048]{2,1,0:T(8,128)(2,1)S(1)} %get-tuple-element.78), channel_id=1, source_target_pairs={{0,10},{1,11},{2,8},{3,9},{4,14},{5,15},{6,12},{7,13},{8,2},{9,3},... | collective-permute-start | bytes 786440 | tf_op jit(solution)/shard_map/ppermute | solution.py:389
  18.5 2.2 %collective-permute-start.3 = (bf16[8,8,2048]{2,1,0:T(8,128)(2,1)S(1)}, bf16[8,8,2048]{2,1,0:T(8,128)(2,1)S(1)}, u32[]{:S(2)}, u32[]{:S(2)}) collective-permute-start(bf16[8,8,2048]{2,1,0:T(8,128)(2,1)S(1)} %get-tuple-element.79), channel_id=1, source_target_pairs={{0,6},{1,7},{2,4},{3,5},{4,2},{5,3},{6,0},{7,1},{8,14},{9,15},{10,... | collective-permute-start | bytes 786440 | tf_op jit(solution)/shard_map/ppermute | solution.py:389
  22.7 3.9 %collective-permute-done.2.refs_2_ = bf16[8,8,2048]{2,1,0:T(8,128)(2,1)S(1)} collective-permute-done((bf16[8,8,2048]{2,1,0:T(8,128)(2,1)S(1)}, bf16[8,8,2048]{2,1,0:T(8,128)(2,1)S(1)}, u32[]{:S(2)}, u32[]{:S(2)}) %collective-permute-start.2) | collective-permute-done | bytes 262176 | tf_op jit(solution)/shard_map/ppermute | solution.py:389
  26.6 2.0 %collective-permute-start.6 = (bf16[8,8,2048]{2,1,0:T(8,128)(2,1)S(1)}, bf16[8,8,2048]{2,1,0:T(8,128)(2,1)S(1)}, u32[]{:S(2)}, u32[]{:S(2)}) collective-permute-start(bf16[8,8,2048]{2,1,0:T(8,128)(2,1)S(1)} %get-tuple-element.82), channel_id=1, source_target_pairs={{0,8},{1,9},{2,10},{3,11},{4,12},{5,13},{6,14},{7,15},{8,0},{9,1},... | collective-permute-start | bytes 786440 | tf_op jit(solution)/shard_map/ppermute | solution.py:389
  28.6 4.1 %collective-permute-done.3.refs_3_ = bf16[8,8,2048]{2,1,0:T(8,128)(2,1)S(1)} collective-permute-done((bf16[8,8,2048]{2,1,0:T(8,128)(2,1)S(1)}, bf16[8,8,2048]{2,1,0:T(8,128)(2,1)S(1)}, u32[]{:S(2)}, u32[]{:S(2)}) %collective-permute-start.3) | collective-permute-done | bytes 262176 | tf_op jit(solution)/shard_map/ppermute | solution.py:389
  32.7 3.4 %collective-permute-start.7 = (bf16[8,8,2048]{2,1,0:T(8,128)(2,1)S(1)}, bf16[8,8,2048]{2,1,0:T(8,128)(2,1)S(1)}, u32[]{:S(2)}, u32[]{:S(2)}) collective-permute-start(bf16[8,8,2048]{2,1,0:T(8,128)(2,1)S(1)} %get-tuple-element.83), channel_id=1, source_target_pairs={{0,4},{1,5},{2,6},{3,7},{4,0},{5,1},{6,2},{7,3},{8,12},{9,13},{10,... | collective-permute-start | bytes 786440 | tf_op jit(solution)/shard_map/ppermute | solution.py:389
  36.1 2.3 %collective-permute-start.1 = (bf16[8,8,2048]{2,1,0:T(8,128)(2,1)S(1)}, bf16[8,8,2048]{2,1,0:T(8,128)(2,1)S(1)}, u32[]{:S(2)}, u32[]{:S(2)}) collective-permute-start(bf16[8,8,2048]{2,1,0:T(8,128)(2,1)S(1)} %get-tuple-element.66), channel_id=1, source_target_pairs={{0,12},{1,13},{2,14},{3,15},{4,8},{5,9},{6,10},{7,11},{8,4},{9,5},... | collective-permute-start | bytes 786440 | tf_op jit(solution)/shard_map/ppermute | solution.py:389
  38.8 2.0 %collective-permute-start.10 = (bf16[8,8,2048]{2,1,0:T(8,128)(2,1)S(1)}, bf16[8,8,2048]{2,1,0:T(8,128)(2,1)S(1)}, u32[]{:S(2)}, u32[]{:S(2)}) collective-permute-start(bf16[8,8,2048]{2,1,0:T(8,128)(2,1)S(1)} %get-tuple-element.85), channel_id=1, source_target_pairs={{0,7},{1,6},{2,5},{3,4},{4,3},{5,2},{6,1},{7,0},{8,15},{9,14},{10,... | collective-permute-start | bytes 786440 | tf_op jit(solution)/shard_map/ppermute | solution.py:389
  40.8 12.3 %collective-permute-done.7.refs_7_ = bf16[8,8,2048]{2,1,0:T(8,128)(2,1)S(1)} collective-permute-done((bf16[8,8,2048]{2,1,0:T(8,128)(2,1)S(1)}, bf16[8,8,2048]{2,1,0:T(8,128)(2,1)S(1)}, u32[]{:S(2)}, u32[]{:S(2)}) %collective-permute-start.7) | collective-permute-done | bytes 262176 | tf_op jit(solution)/shard_map/ppermute | solution.py:389
  53.1 2.6 %collective-permute-start.12 = (bf16[8,8,2048]{2,1,0:T(8,128)(2,1)S(1)}, bf16[8,8,2048]{2,1,0:T(8,128)(2,1)S(1)}, u32[]{:S(2)}, u32[]{:S(2)}) collective-permute-start(bf16[8,8,2048]{2,1,0:T(8,128)(2,1)S(1)} %get-tuple-element.87), channel_id=1, source_target_pairs={{0,3},{1,2},{2,1},{3,0},{4,7},{5,6},{6,5},{7,4},{8,11},{9,10},{10,... | collective-permute-start | bytes 786440 | tf_op jit(solution)/shard_map/ppermute | solution.py:389
  57.5 5.3 %collective-permute-done.11.refs_11_ = bf16[8,8,2048]{2,1,0:T(8,128)(2,1)S(1)} collective-permute-done((bf16[8,8,2048]{2,1,0:T(8,128)(2,1)S(1)}, bf16[8,8,2048]{2,1,0:T(8,128)(2,1)S(1)}, u32[]{:S(2)}, u32[]{:S(2)}) %collective-permute-start.11) | collective-permute-done | bytes 262176 | tf_op jit(solution)/shard_map/ppermute | solution.py:389
  62.8 2.0 %collective-permute-start.15 = (bf16[8,8,2048]{2,1,0:T(8,128)(2,1)S(1)}, bf16[8,8,2048]{2,1,0:T(8,128)(2,1)S(1)}, u32[]{:S(2)}, u32[]{:S(2)}) collective-permute-start(bf16[8,8,2048]{2,1,0:T(8,128)(2,1)S(1)} %get-tuple-element.90), channel_id=1, source_target_pairs={{0,13},{1,12},{2,15},{3,14},{4,9},{5,8},{6,11},{7,10},{8,5},{9,4},... | collective-permute-start | bytes 786440 | tf_op jit(solution)/shard_map/ppermute | solution.py:389
  66.7 4.3 %shard_map.103 = (f32[2,4,16,8,128]{4,3,2,1,0:T(8,128)S(1)}, bf16[2,4,16,8,128]{4,3,2,1,0:T(8,128)(2,1)S(1)}) custom-call(s32[2]{0:T(128)S(1)} %pad_add_fusion.me_ref, bf16[8,128,2048]{2,1,0:T(8,128)(2,1)S(1)} %copy-done.1, bf16[8,128,2048]{2,1,0:T(8,128)(2,1)S(1)} %copy-done), custom_call_target="tpu_custom_call" | custom-call | flops 1073741824 | bytes 8388608 | tf_op jit(solution)/shard_map/pallas_call | solution.py:210
  72.9 5.8 %collective-permute-done.14.refs_14_ = bf16[8,8,2048]{2,1,0:T(8,128)(2,1)S(1)} collective-permute-done((bf16[8,8,2048]{2,1,0:T(8,128)(2,1)S(1)}, bf16[8,8,2048]{2,1,0:T(8,128)(2,1)S(1)}, u32[]{:S(2)}, u32[]{:S(2)}) %collective-permute-start.14) | collective-permute-done | bytes 262176 | tf_op jit(solution)/shard_map/ppermute | solution.py:389
  78.7 4.0 %collective-permute-start.18 = (bf16[2,4,8,2048]{3,2,1,0:T(8,128)(2,1)S(1)}, bf16[2,4,8,2048]{3,2,1,0:T(8,128)(2,1)S(1)}, u32[]{:S(2)}, u32[]{:S(2)}) collective-permute-start(bf16[2,4,8,2048]{3,2,1,0:T(8,128)(2,1)S(1)} %get-tuple-element.96), channel_id=1, source_target_pairs={{0,14},{1,15},{2,12},{3,13},{4,10},{5,11},{6,8},{7,9},{8,6},{9,7},... | collective-permute-start | bytes 786440 | tf_op jit(solution)/shard_map/ppermute | solution.py:389
  82.8 7.4 %shard_map.104 = (bf16[8,128,2048]{2,1,0:T(8,128)(2,1)}, f32[2,4,32,8,128]{4,3,2,1,0:T(8,128)S(1)}, bf16[2,4,32,8,128]{4,3,2,1,0:T(8,128)(2,1)S(1)}) custom-call(s32[2]{0:T(128)S(1)} %pad_add_fusion.me_ref, bf16[8,128,128]{2,1,0:T(8,128)(2,1)S(1)} %copy-done.2, bf16[8,128,2048]{2,1,0:T(8,128)(2,1)S(1)} %copy-done.1, ...), custom_call_target="tpu_custom_call" | custom-call | flops 2147483648 | bytes 12582912 | tf_op jit(solution)/shard_map/pallas_call | solution.py:253
  90.2 4.1 %collective-permute-start.30 = (bf16[2,4,32,8,128]{4,3,2,1,0:T(8,128)(2,1)S(1)}, bf16[2,4,32,8,128]{4,3,2,1,0:T(8,128)(2,1)S(1)}, u32[]{:S(2)}, u32[]{:S(2)}) collective-permute-start(bf16[2,4,32,8,128]{4,3,2,1,0:T(8,128)(2,1)S(1)} %get-tuple-element.111), channel_id=1, source_target_pairs={{0,128},{16,144},{32,160},{48,176},{64,192},{80,208},{96,224},{112... | collective-permute-start | bytes 1572872 | tf_op jit(solution)/shard_map/ppermute | solution.py:356
  95.7 3.5 %collective-permute-start.22 = (bf16[2,4,8,2048]{3,2,1,0:T(8,128)(2,1)S(1)}, bf16[2,4,8,2048]{3,2,1,0:T(8,128)(2,1)S(1)}, u32[]{:S(2)}, u32[]{:S(2)}) collective-permute-start(bf16[2,4,8,2048]{3,2,1,0:T(8,128)(2,1)S(1)} %get-tuple-element.100), channel_id=1, source_target_pairs={{0,12},{1,13},{2,14},{3,15},{4,8},{5,9},{6,10},{7,11},{8,4},{9,5},... | collective-permute-start | bytes 786440 | tf_op jit(solution)/shard_map/ppermute | solution.py:389
  100.7 15.4 %collective-permute-done.21.refs_6_ = bf16[2,4,8,2048]{3,2,1,0:T(8,128)(2,1)S(1)} collective-permute-done((bf16[2,4,8,2048]{3,2,1,0:T(8,128)(2,1)S(1)}, bf16[2,4,8,2048]{3,2,1,0:T(8,128)(2,1)S(1)}, u32[]{:S(2)}, u32[]{:S(2)}) %collective-permute-start.21) | collective-permute-done | bytes 262176 | tf_op jit(solution)/shard_map/ppermute | solution.py:389
  116.1 2.5 %shard_map.105 = (f32[2,4,8,8,128]{4,3,2,1,0:T(8,128)S(1)}, bf16[2,4,8,8,128]{4,3,2,1,0:T(8,128)(2,1)S(1)}) custom-call(s32[2]{0:T(128)S(1)} %pad_add_fusion.me_ref, bf16[8,128,2048]{2,1,0:T(8,128)(2,1)S(1)} %copy-done, bf16[2,4,8,2048]{3,2,1,0:T(8,128)(2,1)S(1)} %get-tuple-element.72.refs_0_, bf16[2,4,8,2048]{3,2,1,0:T(8,128)(2,1)S(1)} %collective-permute-done.16.refs_1_, ...), custom_call_target="tpu_custom_call" | custom-call | flops 536870912 | bytes 4194304 | tf_op jit(solution)/shard_map/pallas_call | solution.py:304
  122.4 3.2 %collective-permute-done.31.refs_3_ = bf16[2,4,8,8,128]{4,3,2,1,0:T(8,128)(2,1)S(1)} collective-permute-done((bf16[2,4,8,8,128]{4,3,2,1,0:T(8,128)(2,1)S(1)}, bf16[2,4,8,8,128]{4,3,2,1,0:T(8,128)(2,1)S(1)}, u32[]{:S(2)}, u32[]{:S(2)}) %collective-permute-start.31) | collective-permute-done | bytes 131104 | tf_op jit(solution)/shard_map/ppermute | solution.py:356
  125.8 3.9 %collective-permute-start.29 = (bf16[2,4,8,2048]{3,2,1,0:T(8,128)(2,1)S(1)}, bf16[2,4,8,2048]{3,2,1,0:T(8,128)(2,1)S(1)}, u32[]{:S(2)}, u32[]{:S(2)}) collective-permute-start(bf16[2,4,8,2048]{3,2,1,0:T(8,128)(2,1)S(1)} %get-tuple-element.110), channel_id=1, source_target_pairs={{0,12},{1,13},{2,14},{3,15},{4,8},{5,9},{6,10},{7,11},{8,4},{9,5},... | collective-permute-start | bytes 786440 | tf_op jit(solution)/shard_map/ppermute | solution.py:389
  131.3 2.8 %collective-permute-done.27.refs_5_ = bf16[2,4,8,2048]{3,2,1,0:T(8,128)(2,1)S(1)} collective-permute-done((bf16[2,4,8,2048]{3,2,1,0:T(8,128)(2,1)S(1)}, bf16[2,4,8,2048]{3,2,1,0:T(8,128)(2,1)S(1)}, u32[]{:S(2)}, u32[]{:S(2)}) %collective-permute-start.27) | collective-permute-done | bytes 262176 | tf_op jit(solution)/shard_map/ppermute | solution.py:389
  134.2 6.0 %collective-permute-done.28.refs_6_ = bf16[2,4,8,2048]{3,2,1,0:T(8,128)(2,1)S(1)} collective-permute-done((bf16[2,4,8,2048]{3,2,1,0:T(8,128)(2,1)S(1)}, bf16[2,4,8,2048]{3,2,1,0:T(8,128)(2,1)S(1)}, u32[]{:S(2)}, u32[]{:S(2)}) %collective-permute-start.28) | collective-permute-done | bytes 262176 | tf_op jit(solution)/shard_map/ppermute | solution.py:389
  140.2 3.1 %shard_map.106 = bf16[16,2,4,8,128]{4,3,2,1,0:T(8,128)(2,1)} custom-call(s32[2]{0:T(128)S(1)} %pad_add_fusion.me_ref, bf16[8,128,2048]{2,1,0:T(8,128)(2,1)S(1)} %copy-done, bf16[2,4,8,2048]{3,2,1,0:T(8,128)(2,1)S(1)} %get-tuple-element.103.refs_0_, bf16[2,4,8,2048]{3,2,1,0:T(8,128)(2,1)S(1)} %collective-permute-done.23.refs_1_, ...), custom_call_target="tpu_custom_call" | custom-call | flops 536870912 | bytes 4194304 | tf_op jit(solution)/shard_map/pallas_call | solution.py:304
  143.4 10.0 %all-to-all-start = ((bf16[16,2,4,8,128]{4,3,2,1,0:T(8,128)(2,1)}), bf16[16,2,4,8,128]{4,3,2,1,0:T(8,128)(2,1)S(1)}, u32[]{:S(2)}, u32[]{:S(2)}) async-start(bf16[16,2,4,8,128]{4,3,2,1,0:T(8,128)(2,1)} %shard_map.106), calls=%async_computation | async-start | bytes 524288 | tf_op jit(solution)/shard_map/all_to_all | solution.py:442
  154.0 5.9 %collective-permute-start.33 = (bf16[2,40,8,128]{3,2,1,0:T(8,128)(2,1)S(1)}, bf16[2,40,8,128]{3,2,1,0:T(8,128)(2,1)S(1)}, u32[]{:S(2)}, u32[]{:S(2)}) collective-permute-start(bf16[2,40,8,128]{3,2,1,0:T(8,128)(2,1)S(1)} %get-tuple-element.116), channel_id=1, source_target_pairs={{0,32},{16,48},{32,0},{48,16},{64,96},{80,112},{96,64},{112,80},{1... | collective-permute-start | bytes 491528 | tf_op jit(solution)/shard_map/ppermute | solution.py:356
  159.9 9.5 %collective-permute-done.33.refs_1_ = bf16[2,40,8,128]{3,2,1,0:T(8,128)(2,1)S(1)} collective-permute-done((bf16[2,40,8,128]{3,2,1,0:T(8,128)(2,1)S(1)}, bf16[2,40,8,128]{3,2,1,0:T(8,128)(2,1)S(1)}, u32[]{:S(2)}, u32[]{:S(2)}) %collective-permute-start.33) | collective-permute-done | bytes 163872 | tf_op jit(solution)/shard_map/ppermute | solution.py:356
  170.2 6.2 %collective-permute-done.34.got_ref = bf16[40,8,128]{2,1,0:T(8,128)(2,1)S(1)} collective-permute-done((bf16[40,8,128]{2,1,0:T(8,128)(2,1)S(1)}, bf16[40,8,128]{2,1,0:T(8,128)(2,1)S(1)}, u32[]{:S(2)}, u32[]{:S(2)}) %collective-permute-start.34) | collective-permute-done | bytes 81952 | tf_op jit(solution)/shard_map/ppermute | solution.py:356
  (59 shorter events, 18.7 us)
Async XLA Ops:
  16.4 48.5 %collective-permute-start = (bf16[8,8,8,2048]{3,2,1,0:T(8,128)(2,1)S(1)}, bf16[8,8,8,2048]{3,2,1,0:T(8,128)(2,1)S(1)}, u32[]{:S(2)}, u32[]{:S(2)}) collective-permute-start(bf16[8,8,8,2048]{3,2,1,0:T(8,128)(2,1)S(1)} %get-tuple-element.71), channel_id=1, source_target_pairs={{0,1},{1,0},{2,3},{3,2},{4,5},{5,4},{6,7},{7,6},{8,9},{9,8},{10,11... | collective-permute-start | bytes 6291464 | tf_op jit(solution)/shard_map/ppermute | solution.py:389
  18.5 14.2 %collective-permute-start.3 = (bf16[8,8,2048]{2,1,0:T(8,128)(2,1)S(1)}, bf16[8,8,2048]{2,1,0:T(8,128)(2,1)S(1)}, u32[]{:S(2)}, u32[]{:S(2)}) collective-permute-start(bf16[8,8,2048]{2,1,0:T(8,128)(2,1)S(1)} %get-tuple-element.79), channel_id=1, source_target_pairs={{0,6},{1,7},{2,4},{3,5},{4,2},{5,3},{6,0},{7,1},{8,14},{9,15},{10,... | collective-permute-start | bytes 786440 | tf_op jit(solution)/shard_map/ppermute | solution.py:389
  20.6 15.4 %collective-permute-start.4 = (bf16[8,8,2048]{2,1,0:T(8,128)(2,1)S(1)}, bf16[8,8,2048]{2,1,0:T(8,128)(2,1)S(1)}, u32[]{:S(2)}, u32[]{:S(2)}) collective-permute-start(bf16[8,8,2048]{2,1,0:T(8,128)(2,1)S(1)} %get-tuple-element.80), channel_id=1, source_target_pairs={{0,14},{1,15},{2,12},{3,13},{4,10},{5,11},{6,8},{7,9},{8,6},{9,7},... | collective-permute-start | bytes 786440 | tf_op jit(solution)/shard_map/ppermute | solution.py:389
  21.7 16.7 %collective-permute-start.5 = (bf16[8,8,2048]{2,1,0:T(8,128)(2,1)S(1)}, bf16[8,8,2048]{2,1,0:T(8,128)(2,1)S(1)}, u32[]{:S(2)}, u32[]{:S(2)}) collective-permute-start(bf16[8,8,2048]{2,1,0:T(8,128)(2,1)S(1)} %get-tuple-element.81), channel_id=1, source_target_pairs={{0,2},{1,3},{2,0},{3,1},{4,6},{5,7},{6,4},{7,5},{8,10},{9,11},{10,... | collective-permute-start | bytes 786440 | tf_op jit(solution)/shard_map/ppermute | solution.py:389
  26.6 12.1 %collective-permute-start.6 = (bf16[8,8,2048]{2,1,0:T(8,128)(2,1)S(1)}, bf16[8,8,2048]{2,1,0:T(8,128)(2,1)S(1)}, u32[]{:S(2)}, u32[]{:S(2)}) collective-permute-start(bf16[8,8,2048]{2,1,0:T(8,128)(2,1)S(1)} %get-tuple-element.82), channel_id=1, source_target_pairs={{0,8},{1,9},{2,10},{3,11},{4,12},{5,13},{6,14},{7,15},{8,0},{9,1},... | collective-permute-start | bytes 786440 | tf_op jit(solution)/shard_map/ppermute | solution.py:389
  32.7 20.4 %collective-permute-start.7 = (bf16[8,8,2048]{2,1,0:T(8,128)(2,1)S(1)}, bf16[8,8,2048]{2,1,0:T(8,128)(2,1)S(1)}, u32[]{:S(2)}, u32[]{:S(2)}) collective-permute-start(bf16[8,8,2048]{2,1,0:T(8,128)(2,1)S(1)} %get-tuple-element.83), channel_id=1, source_target_pairs={{0,4},{1,5},{2,6},{3,7},{4,0},{5,1},{6,2},{7,3},{8,12},{9,13},{10,... | collective-permute-start | bytes 786440 | tf_op jit(solution)/shard_map/ppermute | solution.py:389
  36.1 17.0 %collective-permute-start.1 = (bf16[8,8,2048]{2,1,0:T(8,128)(2,1)S(1)}, bf16[8,8,2048]{2,1,0:T(8,128)(2,1)S(1)}, u32[]{:S(2)}, u32[]{:S(2)}) collective-permute-start(bf16[8,8,2048]{2,1,0:T(8,128)(2,1)S(1)} %get-tuple-element.66), channel_id=1, source_target_pairs={{0,12},{1,13},{2,14},{3,15},{4,8},{5,9},{6,10},{7,11},{8,4},{9,5},... | collective-permute-start | bytes 786440 | tf_op jit(solution)/shard_map/ppermute | solution.py:389
  38.4 17.3 %collective-permute-start.9 = (bf16[8,8,2048]{2,1,0:T(8,128)(2,1)S(1)}, bf16[8,8,2048]{2,1,0:T(8,128)(2,1)S(1)}, u32[]{:S(2)}, u32[]{:S(2)}) collective-permute-start(bf16[8,8,2048]{2,1,0:T(8,128)(2,1)S(1)} %get-tuple-element.84), channel_id=1, source_target_pairs={{0,11},{1,10},{2,9},{3,8},{4,15},{5,14},{6,13},{7,12},{8,3},{9,2},... | collective-permute-start | bytes 786440 | tf_op jit(solution)/shard_map/ppermute | solution.py:389
  38.8 18.2 %collective-permute-start.10 = (bf16[8,8,2048]{2,1,0:T(8,128)(2,1)S(1)}, bf16[8,8,2048]{2,1,0:T(8,128)(2,1)S(1)}, u32[]{:S(2)}, u32[]{:S(2)}) collective-permute-start(bf16[8,8,2048]{2,1,0:T(8,128)(2,1)S(1)} %get-tuple-element.85), channel_id=1, source_target_pairs={{0,7},{1,6},{2,5},{3,4},{4,3},{5,2},{6,1},{7,0},{8,15},{9,14},{10,... | collective-permute-start | bytes 786440 | tf_op jit(solution)/shard_map/ppermute | solution.py:389
  53.1 13.1 %collective-permute-start.12 = (bf16[8,8,2048]{2,1,0:T(8,128)(2,1)S(1)}, bf16[8,8,2048]{2,1,0:T(8,128)(2,1)S(1)}, u32[]{:S(2)}, u32[]{:S(2)}) collective-permute-start(bf16[8,8,2048]{2,1,0:T(8,128)(2,1)S(1)} %get-tuple-element.87), channel_id=1, source_target_pairs={{0,3},{1,2},{2,1},{3,0},{4,7},{5,6},{6,5},{7,4},{8,11},{9,10},{10,... | collective-permute-start | bytes 786440 | tf_op jit(solution)/shard_map/ppermute | solution.py:389
  55.7 15.3 %collective-permute-start.13 = (bf16[8,8,2048]{2,1,0:T(8,128)(2,1)S(1)}, bf16[8,8,2048]{2,1,0:T(8,128)(2,1)S(1)}, u32[]{:S(2)}, u32[]{:S(2)}) collective-permute-start(bf16[8,8,2048]{2,1,0:T(8,128)(2,1)S(1)} %get-tuple-element.88), channel_id=1, source_target_pairs={{0,9},{1,8},{2,11},{3,10},{4,13},{5,12},{6,15},{7,14},{8,1},{9,0},... | collective-permute-start | bytes 786440 | tf_op jit(solution)/shard_map/ppermute | solution.py:389
  57.0 21.7 %collective-permute-start.14 = (bf16[8,8,2048]{2,1,0:T(8,128)(2,1)S(1)}, bf16[8,8,2048]{2,1,0:T(8,128)(2,1)S(1)}, u32[]{:S(2)}, u32[]{:S(2)}) collective-permute-start(bf16[8,8,2048]{2,1,0:T(8,128)(2,1)S(1)} %get-tuple-element.89), channel_id=1, source_target_pairs={{0,5},{1,4},{2,7},{3,6},{4,1},{5,0},{6,3},{7,2},{8,13},{9,12},{10,... | collective-permute-start | bytes 786440 | tf_op jit(solution)/shard_map/ppermute | solution.py:389
  62.8 19.9 %collective-permute-start.15 = (bf16[8,8,2048]{2,1,0:T(8,128)(2,1)S(1)}, bf16[8,8,2048]{2,1,0:T(8,128)(2,1)S(1)}, u32[]{:S(2)}, u32[]{:S(2)}) collective-permute-start(bf16[8,8,2048]{2,1,0:T(8,128)(2,1)S(1)} %get-tuple-element.90), channel_id=1, source_target_pairs={{0,13},{1,12},{2,15},{3,14},{4,9},{5,8},{6,11},{7,10},{8,5},{9,4},... | collective-permute-start | bytes 786440 | tf_op jit(solution)/shard_map/ppermute | solution.py:389
  64.9 17.8 %collective-permute-start.8 = (bf16[8,8,2048]{2,1,0:T(8,128)(2,1)S(1)}, bf16[8,8,2048]{2,1,0:T(8,128)(2,1)S(1)}, u32[]{:S(2)}, u32[]{:S(2)}) collective-permute-start(bf16[8,8,2048]{2,1,0:T(8,128)(2,1)S(1)} %get-tuple-element.68), channel_id=1, source_target_pairs={{0,1},{1,0},{2,3},{3,2},{4,5},{5,4},{6,7},{7,6},{8,9},{9,8},{10,11... | collective-permute-start | bytes 786440 | tf_op jit(solution)/shard_map/ppermute | solution.py:389
  66.1 24.1 %collective-permute-start.16 = (bf16[2,4,8,2048]{3,2,1,0:T(8,128)(2,1)S(1)}, bf16[2,4,8,2048]{3,2,1,0:T(8,128)(2,1)S(1)}, u32[]{:S(2)}, u32[]{:S(2)}) collective-permute-start(bf16[2,4,8,2048]{3,2,1,0:T(8,128)(2,1)S(1)} %get-tuple-element.94), channel_id=1, source_target_pairs={{0,10},{1,11},{2,8},{3,9},{4,14},{5,15},{6,12},{7,13},{8,2},{9,3},... | collective-permute-start | bytes 786440 | tf_op jit(solution)/shard_map/ppermute | solution.py:389
  71.0 23.3 %collective-permute-start.17 = (bf16[2,4,8,2048]{3,2,1,0:T(8,128)(2,1)S(1)}, bf16[2,4,8,2048]{3,2,1,0:T(8,128)(2,1)S(1)}, u32[]{:S(2)}, u32[]{:S(2)}) collective-permute-start(bf16[2,4,8,2048]{3,2,1,0:T(8,128)(2,1)S(1)} %get-tuple-element.95), channel_id=1, source_target_pairs={{0,6},{1,7},{2,4},{3,5},{4,2},{5,3},{6,0},{7,1},{8,14},{9,15},{10,... | collective-permute-start | bytes 786440 | tf_op jit(solution)/shard_map/ppermute | solution.py:389
  78.7 17.0 %collective-permute-start.18 = (bf16[2,4,8,2048]{3,2,1,0:T(8,128)(2,1)S(1)}, bf16[2,4,8,2048]{3,2,1,0:T(8,128)(2,1)S(1)}, u32[]{:S(2)}, u32[]{:S(2)}) collective-permute-start(bf16[2,4,8,2048]{3,2,1,0:T(8,128)(2,1)S(1)} %get-tuple-element.96), channel_id=1, source_target_pairs={{0,14},{1,15},{2,12},{3,13},{4,10},{5,11},{6,8},{7,9},{8,6},{9,7},... | collective-permute-start | bytes 786440 | tf_op jit(solution)/shard_map/ppermute | solution.py:389
  82.7 16.6 %collective-permute-start.19 = (bf16[2,4,8,2048]{3,2,1,0:T(8,128)(2,1)S(1)}, bf16[2,4,8,2048]{3,2,1,0:T(8,128)(2,1)S(1)}, u32[]{:S(2)}, u32[]{:S(2)}) collective-permute-start(bf16[2,4,8,2048]{3,2,1,0:T(8,128)(2,1)S(1)} %get-tuple-element.97), channel_id=1, source_target_pairs={{0,2},{1,3},{2,0},{3,1},{4,6},{5,7},{6,4},{7,5},{8,10},{9,11},{10,... | collective-permute-start | bytes 786440 | tf_op jit(solution)/shard_map/ppermute | solution.py:389
  82.7 17.4 %collective-permute-start.20 = (bf16[2,4,8,2048]{3,2,1,0:T(8,128)(2,1)S(1)}, bf16[2,4,8,2048]{3,2,1,0:T(8,128)(2,1)S(1)}, u32[]{:S(2)}, u32[]{:S(2)}) collective-permute-start(bf16[2,4,8,2048]{3,2,1,0:T(8,128)(2,1)S(1)} %get-tuple-element.98), channel_id=1, source_target_pairs={{0,8},{1,9},{2,10},{3,11},{4,12},{5,13},{6,14},{7,15},{8,0},{9,1},... | collective-permute-start | bytes 786440 | tf_op jit(solution)/shard_map/ppermute | solution.py:389
  90.2 35.6 %collective-permute-start.30 = (bf16[2,4,32,8,128]{4,3,2,1,0:T(8,128)(2,1)S(1)}, bf16[2,4,32,8,128]{4,3,2,1,0:T(8,128)(2,1)S(1)}, u32[]{:S(2)}, u32[]{:S(2)}) collective-permute-start(bf16[2,4,32,8,128]{4,3,2,1,0:T(8,128)(2,1)S(1)} %get-tuple-element.111), channel_id=1, source_target_pairs={{0,128},{16,144},{32,160},{48,176},{64,192},{80,208},{96,224},{112... | collective-permute-start | bytes 1572872 | tf_op jit(solution)/shard_map/ppermute | solution.py:356
  94.3 21.8 %collective-permute-start.21 = (bf16[2,4,8,2048]{3,2,1,0:T(8,128)(2,1)S(1)}, bf16[2,4,8,2048]{3,2,1,0:T(8,128)(2,1)S(1)}, u32[]{:S(2)}, u32[]{:S(2)}) collective-permute-start(bf16[2,4,8,2048]{3,2,1,0:T(8,128)(2,1)S(1)} %get-tuple-element.99), channel_id=1, source_target_pairs={{0,4},{1,5},{2,6},{3,7},{4,0},{5,1},{6,2},{7,3},{8,12},{9,13},{10,... | collective-permute-start | bytes 786440 | tf_op jit(solution)/shard_map/ppermute | solution.py:389
  95.7 20.4 %collective-permute-start.22 = (bf16[2,4,8,2048]{3,2,1,0:T(8,128)(2,1)S(1)}, bf16[2,4,8,2048]{3,2,1,0:T(8,128)(2,1)S(1)}, u32[]{:S(2)}, u32[]{:S(2)}) collective-permute-start(bf16[2,4,8,2048]{3,2,1,0:T(8,128)(2,1)S(1)} %get-tuple-element.100), channel_id=1, source_target_pairs={{0,12},{1,13},{2,14},{3,15},{4,8},{5,9},{6,10},{7,11},{8,4},{9,5},... | collective-permute-start | bytes 786440 | tf_op jit(solution)/shard_map/ppermute | solution.py:389
  99.3 21.1 %collective-permute-start.23 = (bf16[2,4,8,2048]{3,2,1,0:T(8,128)(2,1)S(1)}, bf16[2,4,8,2048]{3,2,1,0:T(8,128)(2,1)S(1)}, u32[]{:S(2)}, u32[]{:S(2)}) collective-permute-start(bf16[2,4,8,2048]{3,2,1,0:T(8,128)(2,1)S(1)} %get-tuple-element.104), channel_id=1, source_target_pairs={{0,10},{1,11},{2,8},{3,9},{4,14},{5,15},{6,12},{7,13},{8,2},{9,3},... | collective-permute-start | bytes 786440 | tf_op jit(solution)/shard_map/ppermute | solution.py:389
  100.1 21.8 %collective-permute-start.24 = (bf16[2,4,8,2048]{3,2,1,0:T(8,128)(2,1)S(1)}, bf16[2,4,8,2048]{3,2,1,0:T(8,128)(2,1)S(1)}, u32[]{:S(2)}, u32[]{:S(2)}) collective-permute-start(bf16[2,4,8,2048]{3,2,1,0:T(8,128)(2,1)S(1)} %get-tuple-element.105), channel_id=1, source_target_pairs={{0,6},{1,7},{2,4},{3,5},{4,2},{5,3},{6,0},{7,1},{8,14},{9,15},{10,... | collective-permute-start | bytes 786440 | tf_op jit(solution)/shard_map/ppermute | solution.py:389
  118.9 11.7 %collective-permute-start.25 = (bf16[2,4,8,2048]{3,2,1,0:T(8,128)(2,1)S(1)}, bf16[2,4,8,2048]{3,2,1,0:T(8,128)(2,1)S(1)}, u32[]{:S(2)}, u32[]{:S(2)}) collective-permute-start(bf16[2,4,8,2048]{3,2,1,0:T(8,128)(2,1)S(1)} %get-tuple-element.106), channel_id=1, source_target_pairs={{0,14},{1,15},{2,12},{3,13},{4,10},{5,11},{6,8},{7,9},{8,6},{9,7},... | collective-permute-start | bytes 786440 | tf_op jit(solution)/shard_map/ppermute | solution.py:389
  120.4 10.9 %collective-permute-start.26 = (bf16[2,4,8,2048]{3,2,1,0:T(8,128)(2,1)S(1)}, bf16[2,4,8,2048]{3,2,1,0:T(8,128)(2,1)S(1)}, u32[]{:S(2)}, u32[]{:S(2)}) collective-permute-start(bf16[2,4,8,2048]{3,2,1,0:T(8,128)(2,1)S(1)} %get-tuple-element.107), channel_id=1, source_target_pairs={{0,2},{1,3},{2,0},{3,1},{4,6},{5,7},{6,4},{7,5},{8,10},{9,11},{10,... | collective-permute-start | bytes 786440 | tf_op jit(solution)/shard_map/ppermute | solution.py:389
  121.9 12.3 %collective-permute-start.27 = (bf16[2,4,8,2048]{3,2,1,0:T(8,128)(2,1)S(1)}, bf16[2,4,8,2048]{3,2,1,0:T(8,128)(2,1)S(1)}, u32[]{:S(2)}, u32[]{:S(2)}) collective-permute-start(bf16[2,4,8,2048]{3,2,1,0:T(8,128)(2,1)S(1)} %get-tuple-element.108), channel_id=1, source_target_pairs={{0,8},{1,9},{2,10},{3,11},{4,12},{5,13},{6,14},{7,15},{8,0},{9,1},... | collective-permute-start | bytes 786440 | tf_op jit(solution)/shard_map/ppermute | solution.py:389
  125.6 14.6 %collective-permute-start.28 = (bf16[2,4,8,2048]{3,2,1,0:T(8,128)(2,1)S(1)}, bf16[2,4,8,2048]{3,2,1,0:T(8,128)(2,1)S(1)}, u32[]{:S(2)}, u32[]{:S(2)}) collective-permute-start(bf16[2,4,8,2048]{3,2,1,0:T(8,128)(2,1)S(1)} %get-tuple-element.109), channel_id=1, source_target_pairs={{0,4},{1,5},{2,6},{3,7},{4,0},{5,1},{6,2},{7,3},{8,12},{9,13},{10,... | collective-permute-start | bytes 786440 | tf_op jit(solution)/shard_map/ppermute | solution.py:389
  125.8 14.4 %collective-permute-start.29 = (bf16[2,4,8,2048]{3,2,1,0:T(8,128)(2,1)S(1)}, bf16[2,4,8,2048]{3,2,1,0:T(8,128)(2,1)S(1)}, u32[]{:S(2)}, u32[]{:S(2)}) collective-permute-start(bf16[2,4,8,2048]{3,2,1,0:T(8,128)(2,1)S(1)} %get-tuple-element.110), channel_id=1, source_target_pairs={{0,12},{1,13},{2,14},{3,15},{4,8},{5,9},{6,10},{7,11},{8,4},{9,5},... | collective-permute-start | bytes 786440 | tf_op jit(solution)/shard_map/ppermute | solution.py:389
  130.5 22.8 %collective-permute-start.32 = (bf16[4,40,8,128]{3,2,1,0:T(8,128)(2,1)S(1)}, bf16[4,40,8,128]{3,2,1,0:T(8,128)(2,1)S(1)}, u32[]{:S(2)}, u32[]{:S(2)}) collective-permute-start(bf16[4,40,8,128]{3,2,1,0:T(8,128)(2,1)S(1)} %get-tuple-element.114), channel_id=1, source_target_pairs={{0,64},{16,80},{32,96},{48,112},{64,0},{80,16},{96,32},{112,48},{1... | collective-permute-start | bytes 983048 | tf_op jit(solution)/shard_map/ppermute | solution.py:356
  143.4 26.8 %all-to-all-start = ((bf16[16,2,4,8,128]{4,3,2,1,0:T(8,128)(2,1)}), bf16[16,2,4,8,128]{4,3,2,1,0:T(8,128)(2,1)S(1)}, u32[]{:S(2)}, u32[]{:S(2)}) async-start(bf16[16,2,4,8,128]{4,3,2,1,0:T(8,128)(2,1)} %shard_map.106), calls=%async_computation | async-start | bytes 524288 | tf_op jit(solution)/shard_map/all_to_all | solution.py:442
  154.0 15.5 %collective-permute-start.33 = (bf16[2,40,8,128]{3,2,1,0:T(8,128)(2,1)S(1)}, bf16[2,40,8,128]{3,2,1,0:T(8,128)(2,1)S(1)}, u32[]{:S(2)}, u32[]{:S(2)}) collective-permute-start(bf16[2,40,8,128]{3,2,1,0:T(8,128)(2,1)S(1)} %get-tuple-element.116), channel_id=1, source_target_pairs={{0,32},{16,48},{32,0},{48,16},{64,96},{80,112},{96,64},{112,80},{1... | collective-permute-start | bytes 491528 | tf_op jit(solution)/shard_map/ppermute | solution.py:356
  (7 other events, 155.7 us)
